TPU v7x, 128 devices: a whole 4x4x4 slice. The times are simulated.
128 devices in a mesh: tile: 8 (over z_lo, x), blk: 16 (over y, z_hi, core).
Axes of the slice: x: 4, y: 4, z: 4 (z_hi: 2, z_lo: 2; z = z_hi * 2 + z_lo), core: 2. Of those that a mesh axis runs over, the one named last changes fastest.
Arguments:
- tiles: bfloat16 [6144, 8, 8, 2048], P(('blk', 'tile')), may hold values from -10 to 10
- w_reduce: bfloat16 [2048, 512], replicated, may hold values from -0.125 to 0.125
- w_spatial: bfloat16 [9, 512, 512], replicated, may hold values from -0.09375 to 0.09375
- w_expand: bfloat16 [512, 2048], replicated, may hold values from -0.25 to 0.25
- w_embed: bfloat16 [2048, 1536], replicated, may hold values from -0.125 to 0.125
- w_query: bfloat16 [1536, 1536], P(None, 'tile'), may hold values from -8 to 8
- w_key: bfloat16 [1536, 1536], P(None, 'tile'), may hold values from -200 to 200
- w_value: bfloat16 [1536, 1536], P(None, 'tile'), may hold values from -0.15625 to 0.15625
- w_out: bfloat16 [1536, 1536], P('tile'), may hold values from -0.15625 to 0.15625
- slide_tiles: int32 [4], replicated, may hold values from 1 to 4608, 6144 in all
Outputs:
- mixed: bfloat16 [6144, 1536], P(('blk', 'tile'))
Inputs may be any that keep to these rules, and one draw needn't show every extreme that they name: `slide_tiles`: the counts sum to 6144 and the largest is exactly 4608.
All inputs are finite; a program needn't handle non-finite values.
Results may differ from a plain program's by a relative error of at most 0.017.
Values may be sent and summed in bfloat16 or wider, within the bound.
A program may use at most 256 MiB of HBM per device.

v0:
```python
import math

import jax
import jax.numpy as jnp
from jax import lax
from jax.sharding import PartitionSpec as P

C = 2048
MID = 512
SIDE = 8
HD = 96


def encode(block, w_reduce, w_spatial, w_expand, w_embed):
    count = block.shape[0]
    flat = block.reshape(count * SIDE * SIDE, C)
    reduced = jax.nn.relu(jnp.dot(flat, w_reduce, preferred_element_type=jnp.float32)).astype(
        jnp.bfloat16
    )
    reduced = reduced.reshape(count, SIDE, SIDE, MID)
    padded = jnp.pad(reduced, ((0, 0), (1, 1), (1, 1), (0, 0)))
    summed = jnp.zeros((count * SIDE * SIDE, MID), jnp.float32)
    for tap in range(9):
        row_off = tap // 3
        col_off = tap % 3
        window = padded[:, row_off : row_off + SIDE, col_off : col_off + SIDE, :].reshape(
            count * SIDE * SIDE, MID
        )
        summed = summed + jnp.dot(window, w_spatial[tap], preferred_element_type=jnp.float32)
    spatial = jax.nn.relu(summed).astype(jnp.bfloat16)
    output = jax.nn.relu(
        flat.astype(jnp.float32) + jnp.dot(spatial, w_expand, preferred_element_type=jnp.float32)
    )
    pooled = (jnp.sum(output.reshape(count, SIDE * SIDE, C), axis=1) / (SIDE * SIDE)).astype(
        jnp.bfloat16
    )
    return jnp.dot(pooled, w_embed, preferred_element_type=jnp.float32).astype(jnp.bfloat16)


def normalize(rows):
    values = rows.astype(jnp.float32)
    center = jnp.mean(values, axis=1, keepdims=True)
    spread = jnp.mean((values - center) ** 2, axis=1, keepdims=True)
    return ((values - center) * lax.rsqrt(spread + 1e-05)).astype(jnp.bfloat16)


def slide_of(positions, slide_tiles):
    ends = jnp.cumsum(slide_tiles)[:-1]
    return jnp.sum((positions[:, None] >= ends[None, :]).astype(jnp.int32), axis=1)


def shards(
    tiles, w_reduce, w_spatial, w_expand, w_embed, w_query, w_key, w_value, w_out, slide_tiles
):
    emb = encode(tiles, w_reduce, w_spatial, w_expand, w_embed)
    width = w_query.shape[1]
    heads_here = width // HD
    w_joined = jnp.concatenate([w_query, w_key, w_value], axis=1)
    joined = jnp.dot(
        normalize(lax.all_gather(emb, "tile", axis=0, tiled=True)),
        w_joined,
        preferred_element_type=jnp.float32,
    ).astype(jnp.bfloat16)
    length = joined.shape[0]
    query = joined[:, :width].reshape(length, heads_here, HD)
    key_value = joined[:, width:]
    query_pos = lax.axis_index("blk") * length + jnp.arange(length, dtype=jnp.int32)
    query_slide = slide_of(query_pos, slide_tiles)
    scale = 1.0 / math.sqrt(HD)
    piece = lax.all_gather(key_value, "blk", axis=0, tiled=True)
    rows = piece.shape[0]
    key_pos = jnp.arange(rows, dtype=jnp.int32)
    same = query_slide[:, None] == slide_of(key_pos, slide_tiles)[None, :]
    top_old = jnp.full((heads_here, length), -1e30, jnp.float32)
    keys = piece[:, :width].reshape(rows, heads_here, HD)
    values = piece[:, width:].reshape(rows, heads_here, HD)
    scores = jnp.einsum("qhd,khd->hqk", query, keys, preferred_element_type=jnp.float32) * scale
    scores = jnp.where(same[None], scores, -1e30)
    top_new = jnp.maximum(top_old, jnp.max(scores, axis=2))
    probs = jnp.where(same[None], jnp.exp(scores - top_new[:, :, None]), 0.0)
    total_new = jnp.sum(probs, axis=2)
    accum_new = jnp.einsum(
        "hqk,khd->hqd", probs.astype(jnp.bfloat16), values, preferred_element_type=jnp.float32
    )
    attended = (
        (accum_new / total_new[:, :, None])
        .transpose(1, 0, 2)
        .reshape(length, width)
        .astype(jnp.bfloat16)
    )
    summed = lax.psum_scatter(
        jnp.dot(attended, w_out, preferred_element_type=jnp.float32).astype(jnp.bfloat16),
        "tile",
        scatter_dimension=0,
        tiled=True,
    ).astype(jnp.float32)
    return (emb.astype(jnp.float32) + summed).astype(jnp.bfloat16)


def solution(mesh):
    placed = (
        P(("blk", "tile"), None, None, None),
        P(),
        P(),
        P(),
        P(),
        P(None, "tile"),
        P(None, "tile"),
        P(None, "tile"),
        P("tile", None),
        P(),
    )
    return jax.shard_map(
        shards, mesh=mesh, in_specs=placed, out_specs=P(("blk", "tile"), None), check_vma=False
    )
```

profile of v0, /device:TPU:8, one launch (start us, length us, event | category | flops | bytes accessed | tf_op | source)
XLA Modules:
  0.0 305.8 jit_solution(4576410972492332639)
XLA Ops:
  6.5 0.0 copy-start
  6.5 0.0 all-gather.3.cloned.1.call-start
  6.5 13.1 %maximum_convert_fusion.1 = bf16[3072,512]{1,0:T(8,128)(2,1)} fusion(bf16[3072,2048]{1,0:T(8,128)(2,1)} %bitcast.73, bf16[2048,512]{1,0:T(8,128)(2,1)} %param.11), kind=kOutput, calls=%fused_computation.17 | convolution fusion | flops 6445596672 | bytes 17825792 | tf_op jit(solution)/shard_map/dot_general | solution.py:17
  19.6 13.5 %pad_slice_fusion = (bf16[48,8,8,512]{3,2,1,0:T(8,128)(2,1)}, bf16[48,8,8,512]{3,2,1,0:T(8,128)(2,1)S(1)}, bf16[48,8,8,512]{3,2,1,0:T(8,128)(2,1)S(1)}, bf16[48,...) fusion(bf16[48,8,8,512]{3,2,1,0:T(8,128)(2,1)} %bitcast.83), kind=kLoop, calls=%fused_computation.3 | loop fusion | bytes 28311552 | tf_op jit(solution)/shard_map/slice | solution.py:26
  33.1 0.0 copy-start.3
  33.1 0.0 copy-start.4
  33.1 6.6 %fusion.40 = f32[3072,512]{1,0:T(8,128)} fusion(bf16[3072,512]{1,0:T(8,128)(2,1)} %maximum_convert_fusion.1, bf16[9,512,512]{2,1,0:T(8,128)(2,1)} %param.12), kind=kOutput, calls=%fused_computation.46 | convolution fusion | flops 1610612736 | bytes 9961472 | tf_op jit(solution)/shard_map/dot_general | solution.py:29
  39.8 0.0 copy-done.3
  39.8 0.0 copy-done.4
  39.8 4.5 %fusion.34 = f32[3072,512]{1,0:T(8,128)} fusion(bf16[3072,512]{1,0:T(8,128)(2,1)S(1)} %bitcast.82, bf16[9,512,512]{2,1,0:T(8,128)(2,1)S(1)} %copy-done.4), kind=kOutput, calls=%fused_computation.40 | convolution fusion | flops 1610612736 | bytes 9961472 | tf_op jit(solution)/shard_map/dot_general | solution.py:29
  44.3 4.5 %fusion.36 = f32[3072,512]{1,0:T(8,128)} fusion(bf16[3072,512]{1,0:T(8,128)(2,1)S(1)} %bitcast.81, bf16[9,512,512]{2,1,0:T(8,128)(2,1)S(1)} %copy-done.4), kind=kOutput, calls=%fused_computation.42 | convolution fusion | flops 1610612736 | bytes 9961472 | tf_op jit(solution)/shard_map/dot_general | solution.py:29
  48.8 4.4 %fusion.38 = f32[3072,512]{1,0:T(8,128)} fusion(bf16[3072,512]{1,0:T(8,128)(2,1)S(1)} %bitcast.80, bf16[9,512,512]{2,1,0:T(8,128)(2,1)S(1)} %copy-done.4), kind=kOutput, calls=%fused_computation.44 | convolution fusion | flops 1610612736 | bytes 9961472 | tf_op jit(solution)/shard_map/dot_general | solution.py:29
  53.2 4.4 %fusion.42 = f32[3072,512]{1,0:T(8,128)} fusion(bf16[3072,512]{1,0:T(8,128)(2,1)S(1)} %bitcast.79, bf16[9,512,512]{2,1,0:T(8,128)(2,1)S(1)} %copy-done.4), kind=kOutput, calls=%fused_computation.48 | convolution fusion | flops 1610612736 | bytes 9961472 | tf_op jit(solution)/shard_map/dot_general | solution.py:29
  57.7 4.5 %fusion.44 = f32[3072,512]{1,0:T(8,128)} fusion(bf16[3072,512]{1,0:T(8,128)(2,1)S(1)} %bitcast.78, bf16[9,512,512]{2,1,0:T(8,128)(2,1)S(1)} %copy-done.4), kind=kOutput, calls=%fused_computation.50 | convolution fusion | flops 1610612736 | bytes 9961472 | tf_op jit(solution)/shard_map/dot_general | solution.py:29
  62.1 4.4 %fusion.46 = f32[3072,512]{1,0:T(8,128)} fusion(bf16[3072,512]{1,0:T(8,128)(2,1)S(1)} %bitcast.77, bf16[9,512,512]{2,1,0:T(8,128)(2,1)S(1)} %copy-done.4), kind=kOutput, calls=%fused_computation.52 | convolution fusion | flops 1610612736 | bytes 9961472 | tf_op jit(solution)/shard_map/dot_general | solution.py:29
  66.5 4.5 %fusion.48 = f32[3072,512]{1,0:T(8,128)} fusion(bf16[3072,512]{1,0:T(8,128)(2,1)S(1)} %bitcast.76, bf16[9,512,512]{2,1,0:T(8,128)(2,1)S(1)} %copy-done.4), kind=kOutput, calls=%fused_computation.54 | convolution fusion | flops 1610612736 | bytes 9961472 | tf_op jit(solution)/shard_map/dot_general | solution.py:29
  71.0 0.0 copy-done
  71.0 33.0 %add_maximum_fusion = f32[3072,2048]{1,0:T(8,128)} fusion(bf16[3072,2048]{1,0:T(8,128)(2,1)} %bitcast.74, bf16[512,2048]{1,0:T(8,128)(2,1)S(1)} %copy-done, f32[3072,512]{1,0:T(8,128)} %fusion.34, f32[3072,512]{1,0:T(8,128)} %fusion.36, f32[3072,512]{1,0:T(8,128)} %fusion.38, f32[3072,512]{1,0:T(8,128)} %fusion.40, f32[3072,512]{1,0:T(8,128)} %fusion.42, ...), kind=kOutput, calls=%fused_computation | convolution fusion | flops 8087666688 | bytes 93847552 | tf_op jit(solution)/shard_map/dot_general | solution.py:32
  104.0 9.5 %reduce_sum.54 = f32[48,2048]{1,0:T(8,128)S(1)} reduce(f32[48,64,2048]{2,1,0:T(8,128)} %bitcast.72, f32[]{:T(128)} %constant.11.clone.1), dimensions={1}, to_apply=%region_0.1 | reduce | flops 6193152 | bytes 25559044 | tf_op jit(solution)/shard_map/reduce_sum | solution.py:34
  113.6 0.0 copy-start.7
  113.6 0.0 copy-start.8
  113.6 0.0 copy-start.9
  113.6 4.7 %convolution_convert_fusion.1 = bf16[48,1536]{1,0:T(8,128)(2,1)} fusion(bf16[2048,1536]{1,0:T(8,128)(2,1)} %param.14, f32[48,2048]{1,0:T(8,128)S(1)} %reduce_sum.54), kind=kOutput, calls=%fused_computation.26 | convolution fusion | flops 302260224 | bytes 6832128 | tf_op jit(solution)/shard_map/dot_general | solution.py:37
  118.3 0.0 all-gather.3.cloned.1.call-update
  118.3 0.0 all-gather.5.cloned.1.call-start
  118.4 41.6 %all-gather.3.cloned.1.call-done = bf16[384,1536]{1,0:T(8,128)(2,1)} async-done(((bf16[48,1536]{1,0:T(8,128)(2,1)}), bf16[384,1536]{1,0:T(8,128)(2,1)}) %all-gather.3.cloned.1.call-update) | async-done | bytes 1179664 | tf_op jit(solution)/shard_map/all_gather | solution.py:60
  160.0 1.5 convert_reduce_fusion
  161.5 1.7 fusion.8
  163.2 0.0 copy-done.7
  163.2 0.0 copy-done.8
  163.3 0.0 copy-done.9
  163.3 0.0 copy-start.10
  163.3 2.5 fusion.16
  165.8 0.7 slice.92
  166.5 0.0 all-gather.5.cloned.1.call-update
  166.6 0.0 reduce-scatter.2.cloned.1.call-start
  166.6 0.0 copy-done.10
  166.6 0.2 reduce-window.4
  166.8 0.1 convert_reduce_fusion.2
  166.9 0.1 convert_reduce_fusion.1
  167.0 2.9 broadcast_compare_fusion
  169.9 57.3 %all-gather.5.cloned.1.call-done = bf16[6144,384]{0,1:T(8,128)(2,1)} async-done(((bf16[384,384]{0,1:T(8,128)(2,1)}), bf16[6144,384]{0,1:T(8,128)(2,1)}) %all-gather.5.cloned.1.call-update) | async-done | bytes 4718608 | tf_op jit(solution)/shard_map/all_gather | solution.py:70
  227.2 5.1 %fusion.67 = (bf16[6144,192]{0,1:T(8,128)(2,1)}, bf16[6144,192]{0,1:T(8,128)(2,1)}) fusion(bf16[6144,384]{0,1:T(8,128)(2,1)} %all-gather.5.cloned.1.call-done), kind=kLoop, calls=%fused_computation.82 | loop fusion | bytes 9437184 | tf_op jit(solution)/shard_map/slice | solution.py:75
  232.3 6.4 %fusion = (f32[2,384]{1,0:T(2,128)S(1)}, f32[2,384,6144]{2,1,0:T(8,128)S(1)}) fusion(pred[384,6144]{1,0:T(8,128)(4,1)} %broadcast_compare_fusion, bf16[384,2,96]{0,2,1:T(8,128)(2,1)S(1)} %bitcast.86, bf16[6144,2,96]{0,2,1:T(8,128)(2,1)} %bitcast.85), kind=kOutput, calls=%fused_computation.11 | convolution fusion | flops 920124672 | bytes 23743488 | tf_op jit(solution)/shard_map/qhd,khd->hqk/dot_general | solution.py:77
  238.7 0.0 copy-start.2
  238.7 8.0 %fusion.1 = f32[2,384]{1,0:T(2,128)S(1)} fusion(f32[2,384,6144]{2,1,0:T(8,128)S(1)} %get-tuple-element.16, f32[2,384]{1,0:T(2,128)S(1)} %broadcast_maximum_fusion, pred[384,6144]{1,0:T(8,128)(4,1)} %broadcast_compare_fusion), kind=kLoop, calls=%fused_computation.12 | loop fusion | flops 23592192 | bytes 21239808 | tf_op jit(solution)/shard_map/reduce_sum | solution.py:81
  246.7 0.0 copy-done.2
  246.7 0.0 copy-start.6
  246.7 0.0 copy-start.5
  246.8 0.0 copy-start.1
  246.8 10.9 %fusion.28 = bf16[384,2,96]{0,2,1:T(8,128)(2,1)S(1)} fusion(bf16[6144,2,96]{0,2,1:T(8,128)(2,1)} %bitcast.84, f32[2,384,6144]{2,1,0:T(8,128)} %copy-done.2, f32[2,384]{1,0:T(2,128)S(1)} %broadcast_maximum_fusion, pred[384,6144]{1,0:T(8,128)(4,1)} %broadcast_compare_fusion, f32[384,2]{0,1:T(2,128)S(1)} %bitcast.88), kind=kOutput, calls=%fused_computation.38 | convolution fusion | flops 929710080 | bytes 23746560 | tf_op jit(solution)/shard_map/hqk,khd->hqd/dot_general | solution.py:82
  257.7 0.0 copy-done.6
  257.7 1.5 convolution_convert_fusion
  259.2 0.0 reduce-scatter.2.cloned.1.call-update
  259.2 38.4 %reduce-scatter.2.cloned.1.call-done = bf16[48,1536]{1,0:T(8,128)(2,1)} async-done(((bf16[384,1536]{1,0:T(8,128)(2,1)}), bf16[48,1536]{1,0:T(8,128)(2,1)}) %reduce-scatter.2.cloned.1.call-update) | async-done | bytes 147472 | tf_op jit(solution)/shard_map/reduce_scatter | solution.py:91
  297.6 0.0 copy-done.5
  297.6 1.6 add_convert_fusion
  299.3 0.0 copy-done.1
  (6 shorter events, 0.0 us)
Async XLA Ops:
  6.5 64.5 %copy-start = (bf16[512,2048]{1,0:T(8,128)(2,1)S(1)}, bf16[512,2048]{1,0:T(8,128)(2,1)}, u32[]{:S(2)}) copy-start(bf16[512,2048]{1,0:T(8,128)(2,1)} %param.13) | copy-start | bytes 6291460
  6.5 153.5 %all-gather.3.cloned.1.call-start = ((), (), s32[]{:S(2)}) async-start(), calls=%async_computation.1 | async-start | bytes 1327104 | tf_op jit(solution)/shard_map/all_gather | solution.py:60
  33.1 6.7 %copy-start.3 = (bf16[48,8,8,512]{3,2,1,0:T(8,128)(2,1)S(1)}, bf16[48,8,8,512]{3,2,1,0:T(8,128)(2,1)}, u32[]{:S(2)}) copy-start(bf16[48,8,8,512]{3,2,1,0:T(8,128)(2,1)} %get-tuple-element.13) | copy-start | bytes 9437188
  33.1 6.7 %copy-start.4 = (bf16[9,512,512]{2,1,0:T(8,128)(2,1)S(1)}, bf16[9,512,512]{2,1,0:T(8,128)(2,1)}, u32[]{:S(2)}) copy-start(bf16[9,512,512]{2,1,0:T(8,128)(2,1)} %param.12) | copy-start | bytes 14155780
  113.6 49.7 %copy-start.7 = (bf16[1536,192]{0,1:T(8,128)(2,1)S(1)}, bf16[1536,192]{0,1:T(8,128)(2,1)}, u32[]{:S(2)}) copy-start(bf16[1536,192]{0,1:T(8,128)(2,1)} %param.17) | copy-start | bytes 1769476
  113.6 49.7 %copy-start.8 = (bf16[1536,192]{0,1:T(8,128)(2,1)S(1)}, bf16[1536,192]{0,1:T(8,128)(2,1)}, u32[]{:S(2)}) copy-start(bf16[1536,192]{0,1:T(8,128)(2,1)} %param.16) | copy-start | bytes 1769476
  113.6 49.7 %copy-start.9 = (bf16[1536,192]{0,1:T(8,128)(2,1)S(1)}, bf16[1536,192]{0,1:T(8,128)(2,1)}, u32[]{:S(2)}) copy-start(bf16[1536,192]{0,1:T(8,128)(2,1)} %param.15) | copy-start | bytes 1769476
  118.3 108.9 %all-gather.5.cloned.1.call-start = ((), (), s32[]{:S(2)}) async-start(), calls=%async_computation.2 | async-start | bytes 5013504 | tf_op jit(solution)/shard_map/all_gather | solution.py:70
  163.3 3.3 %copy-start.10 = (s32[4]{0:T(128)S(1)}, s32[4]{0:T(128)}, u32[]{:S(2)}) copy-start(s32[4]{0:T(128)} %param.19) | copy-start | bytes 52
  166.6 131.1 %reduce-scatter.2.cloned.1.call-start = ((), (), s32[]{:S(2)}) async-start(), calls=%async_computation.3 | async-start | bytes 1327104 | tf_op jit(solution)/shard_map/reduce_scatter | solution.py:91
  238.7 8.0 %copy-start.2 = (f32[2,384,6144]{2,1,0:T(8,128)}, f32[2,384,6144]{2,1,0:T(8,128)S(1)}, u32[]{:S(2)}) copy-start(f32[2,384,6144]{2,1,0:T(8,128)S(1)} %get-tuple-element.16) | copy-start | bytes 56623108
  246.7 10.9 %copy-start.6 = (bf16[192,1536]{1,0:T(8,128)(2,1)S(1)}, bf16[192,1536]{1,0:T(8,128)(2,1)}, u32[]{:S(2)}) copy-start(bf16[192,1536]{1,0:T(8,128)(2,1)} %param.18) | copy-start | bytes 1769476
  246.7 50.9 %copy-start.5 = (bf16[48,1536]{1,0:T(8,128)(2,1)S(1)}, bf16[48,1536]{1,0:T(8,128)(2,1)}, u32[]{:S(2)}) copy-start(bf16[48,1536]{1,0:T(8,128)(2,1)} %convolution_convert_fusion.1) | copy-start | bytes 442372
  246.8 52.5 %copy-start.1 = (bf16[512,2048]{1,0:T(8,128)(2,1)S(1)}, bf16[512,2048]{1,0:T(8,128)(2,1)}, u32[]{:S(2)}) copy-start(bf16[512,2048]{1,0:T(8,128)(2,1)} %param.13) | copy-start | bytes 6291460
Sparse Core Ops, SparseCore 0:
  118.4 41.5 all-gather.2
  166.7 60.4 all-gather.4
  259.3 38.2 reduce-scatter.1
where the time goes:
time: 306 us
  waiting for transfers between devices  137 us (45%)
  matrix products  110 us (36%)
  other arithmetic  25.6 us (8%)
  local copies, waits for them, and re-layouts  19.4 us (6%)
  between operations  13.3 us (4%)
    all_gather x1, waiting for transfers between devices, shards(): piece = lax.all_gather(key_value, 'blk', axis=0, tiled=True)  57.3 us
    all_gather x1, waiting for transfers between devices, shards(): lax.all_gather(emb, 'tile', axis=0, tiled=True)  41.6 us
    reduce_scatter x1, waiting for transfers between devices, shards(): lax.psum_scatter(jnp.dot(attended, w_out, preferred_element_type=jnp.floa...  38.4 us
    dot_general x8, matrix products, encode(): jnp.dot(window, w_spatial[tap], preferred_element_type=jnp.float32)  37.9 us
    dot_general x1, matrix products, encode(): jnp.dot(spatial, w_expand, preferred_element_type=jnp.float32)  33 us
    slice x1, local copies, waits for them, and re-layouts, encode(): padded[:, row_off:row_off + SIDE, col_off:col_off + SIDE, :]  13.5 us
    dot_general x1, matrix products, encode(): jnp.dot(flat, w_reduce, preferred_element_type=jnp.float32)  13.1 us
    dot_general x1, matrix products, shards(): jnp.einsum('hqk,khd->hqd', probs.astype(jnp.bfloat16), values, preferred_...  10.9 us
  transfers between devices with their start and end apart: 3, of which 3 were waited for; matrix products, arithmetic and copies ran while one was open for 1% of the time, Pallas kernels for 0%

commit v1 on v0

--- a/solution.py
+++ b/solution.py
@@ -3,6 +3,8 @@
 import jax
 import jax.numpy as jnp
 from jax import lax
+from jax.experimental import pallas as pl
+from jax.experimental.pallas import tpu as pltpu
 from jax.sharding import PartitionSpec as P
 
 C = 2048
@@ -11,30 +13,67 @@
 HD = 96
 
 
-def encode(block, w_reduce, w_spatial, w_expand, w_embed):
-    count = block.shape[0]
-    flat = block.reshape(count * SIDE * SIDE, C)
-    reduced = jax.nn.relu(jnp.dot(flat, w_reduce, preferred_element_type=jnp.float32)).astype(
-        jnp.bfloat16
-    )
-    reduced = reduced.reshape(count, SIDE, SIDE, MID)
-    padded = jnp.pad(reduced, ((0, 0), (1, 1), (1, 1), (0, 0)))
-    summed = jnp.zeros((count * SIDE * SIDE, MID), jnp.float32)
-    for tap in range(9):
-        row_off = tap // 3
-        col_off = tap % 3
-        window = padded[:, row_off : row_off + SIDE, col_off : col_off + SIDE, :].reshape(
-            count * SIDE * SIDE, MID
-        )
-        summed = summed + jnp.dot(window, w_spatial[tap], preferred_element_type=jnp.float32)
-    spatial = jax.nn.relu(summed).astype(jnp.bfloat16)
-    output = jax.nn.relu(
-        flat.astype(jnp.float32) + jnp.dot(spatial, w_expand, preferred_element_type=jnp.float32)
-    )
-    pooled = (jnp.sum(output.reshape(count, SIDE * SIDE, C), axis=1) / (SIDE * SIDE)).astype(
-        jnp.bfloat16
-    )
-    return jnp.dot(pooled, w_embed, preferred_element_type=jnp.float32).astype(jnp.bfloat16)
+T = 16
+R = T * 64
+VMEM_LIMIT = 60 << 20
+
+
+def encode_body(x_ref, wr_ref, ws_ref, wx_ref, we_ref, o_ref, p_ref, pool_ref):
+    g = pl.program_id(0)
+
+    @pl.when(g == 0)
+    def _():
+        p_ref[:, 0] = jnp.zeros((T, 8, 1536), jnp.bfloat16)
+        p_ref[:, 9] = jnp.zeros((T, 8, 1536), jnp.bfloat16)
+
+    x = x_ref[...].reshape(R, C)
+    r = jnp.maximum(jnp.dot(x, wr_ref[...], preferred_element_type=jnp.float32), 0.0)
+    j = lax.broadcasted_iota(jnp.int32, (R, MID), 0) % 8
+    left = jnp.where(j == 0, 0.0, pltpu.roll(r, 1, 0))
+    right = jnp.where(j == 7, 0.0, pltpu.roll(r, R - 1, 0))
+    for at, shifted in enumerate((left, r, right)):
+        p_ref[:, 1:9, :, at * MID : (at + 1) * MID] = shifted.astype(jnp.bfloat16).reshape(T, 8, 8, MID)
+    acc = jnp.dot(p_ref[:, 0:8].reshape(R, 3 * MID), ws_ref[0], preferred_element_type=jnp.float32)
+    acc += jnp.dot(p_ref[:, 1:9].reshape(R, 3 * MID), ws_ref[1], preferred_element_type=jnp.float32)
+    acc += jnp.dot(p_ref[:, 2:10].reshape(R, 3 * MID), ws_ref[2], preferred_element_type=jnp.float32)
+    s = jnp.maximum(acc, 0.0).astype(jnp.bfloat16)
+    for c in range(4):
+        cols = slice(c * 512, (c + 1) * 512)
+        y = jnp.dot(s, wx_ref[:, cols], preferred_element_type=jnp.float32)
+        y = jnp.maximum(y + x_ref[:, :, :, cols].reshape(R, 512).astype(jnp.float32), 0.0)
+        y = jnp.sum(jnp.sum(y.reshape(T, 8, 8, 512), axis=1), axis=1) * (1.0 / 64)
+        pool_ref[pl.ds(pl.multiple_of(g * T, T), T), cols] = y
+
+    @pl.when(g == pl.num_programs(0) - 1)
+    def _():
+        o_ref[...] = jnp.dot(
+            pool_ref[...].astype(jnp.bfloat16), we_ref[...], preferred_element_type=jnp.float32
+        ).astype(jnp.bfloat16)
+
+
+def encode(tiles, w_reduce, w_spatial, w_expand, w_embed):
+    def full(s):
+        return pl.BlockSpec(s, lambda g: (0,) * len(s), pipeline_mode=pl.Buffered(1))
+
+    return pl.pallas_call(
+        encode_body,
+        grid=(48 // T,),
+        in_specs=[
+            pl.BlockSpec((T, 8, 8, C), lambda g: (g, 0, 0, 0)),
+            full((C, MID)),
+            full((3, 3 * MID, MID)),
+            full((MID, C)),
+            full((C, 1536)),
+        ],
+        out_specs=pl.BlockSpec((48, 1536), lambda g: (0, 0)),
+        out_shape=jax.ShapeDtypeStruct((48, 1536), jnp.bfloat16),
+        scratch_shapes=[
+            pltpu.VMEM((T, 10, 8, 3 * MID), jnp.bfloat16),
+            pltpu.VMEM((48, C), jnp.float32),
+        ],
+        compiler_params=pltpu.CompilerParams(vmem_limit_bytes=VMEM_LIMIT),
+        name="encode",
+    )(tiles, w_reduce, w_spatial.reshape(3, 3 * MID, MID), w_expand, w_embed)
 
 
 def normalize(rows):

time: 306 us -> 230 us (0.75)
  matrix products: 110 us -> 20.2 us
  Pallas kernels: 0 us -> 38.6 us
  local copies, waits for them, and re-layouts: 19.4 us -> 5.85 us
  other arithmetic: 25.6 us -> 13.2 us
    dot_general x11 -> x0, matrix products: 88.7 us -> none  [the longest x8 37.9 us: encode(): jnp.dot(window, w_spatial[tap], preferred_element_type=jnp.float32)]
    pallas_call x0 -> x1, Pallas kernels: none -> 38.6 us  [encode(): pl.pallas_call(encode_body, grid=(48 // T,), in_specs=[pl.BlockSpec((T, 8...]
    slice x1 -> x0, local copies, waits for them, and re-layouts: 13.5 us -> none  [encode(): padded[:, row_off:row_off + SIDE, col_off:col_off + SIDE, :]]
    reduce_sum x1 -> x0, other arithmetic: 9.51 us -> none  [encode(): jnp.sum(output.reshape(count, SIDE * SIDE, C), axis=1) / (SIDE * SIDE)]
where the time goes in v1:
time: 230 us
  waiting for transfers between devices  139 us (60%)
  Pallas kernels  38.6 us (17%)
  matrix products  20.2 us (9%)
  between operations  13.3 us (6%)
  other arithmetic  13.2 us (6%)
  local copies, waits for them, and re-layouts  5.85 us (3%)
    all_gather x1, waiting for transfers between devices, shards(): piece = lax.all_gather(key_value, 'blk', axis=0, tiled=True)  58.5 us
    all_gather x1, waiting for transfers between devices, shards(): lax.all_gather(emb, 'tile', axis=0, tiled=True)  41.6 us
    pallas_call x1, Pallas kernels, encode(): pl.pallas_call(encode_body, grid=(48 // T,), in_specs=[pl.BlockSpec((T, 8...  38.6 us
    reduce_scatter x1, waiting for transfers between devices, shards(): lax.psum_scatter(jnp.dot(attended, w_out, preferred_element_type=jnp.floa...  38.5 us
    dot_general x1, matrix products, shards(): jnp.einsum('hqk,khd->hqd', probs.astype(jnp.bfloat16), values, preferred_...  10.1 us
    reduce_sum x1, other arithmetic, shards(): total_new = jnp.sum(probs, axis=2)  6.46 us
    dot_general x1, matrix products, shards(): jnp.einsum('qhd,khd->hqk', query, keys, preferred_element_type=jnp.float32)  6.1 us
    slice x1, local copies, waits for them, and re-layouts, shards(): keys = piece[:, :width].reshape(rows, heads_here, HD)  5.06 us
  transfers between devices with their start and end apart: 3, of which 3 were waited for; matrix products, arithmetic and copies ran while one was open for 1% of the time, Pallas kernels for 0%

profile of v1, /device:TPU:8, one launch (start us, length us, event | category | flops | bytes accessed | tf_op | source)
XLA Modules:
  0.0 230.0 jit_solution(1628266946149187425)
XLA Ops:
  6.5 0.0 copy-start
  6.5 0.0 all-gather.3.cloned.1.call-start
  6.5 0.0 copy-start.3
  6.5 0.0 copy-start.4
  6.5 0.0 copy-start.5
  6.6 38.6 %encode.1 = bf16[48,1536]{1,0:T(8,128)(2,1)} custom-call(bf16[48,8,8,2048]{3,2,1,0:T(8,128)(2,1)} %x_ref.1, bf16[2048,512]{1,0:T(8,128)(2,1)} %wr_ref.1, bf16[3,1536,512]{2,1,0:T(8,128)(2,1)} %bitcast.20, bf16[512,2048]{1,0:T(8,128)(2,1)} %wx_ref.1, bf16[2048,1536]{1,0:T(8,128)(2,1)} %we_ref.1), custom_call_target="tpu_custom_call" | custom-call | tf_op jit(solution)/shard_map/encode/pallas_call | solution.py:58
  45.2 0.0 all-gather.3.cloned.1.call-update
  45.2 0.0 all-gather.5.cloned.1.call-start
  45.3 41.6 %all-gather.3.cloned.1.call-done = bf16[384,1536]{1,0:T(8,128)(2,1)} async-done(((bf16[48,1536]{1,0:T(8,128)(2,1)}), bf16[384,1536]{1,0:T(8,128)(2,1)}) %all-gather.3.cloned.1.call-update) | async-done | bytes 1179664 | tf_op jit(solution)/shard_map/all_gather | solution.py:99
  86.9 1.5 convert_reduce_fusion
  88.4 1.7 fusion.8
  90.1 0.0 copy-done.3
  90.1 0.0 copy-done.4
  90.2 0.0 copy-done.5
  90.2 0.0 copy-start.6
  90.2 2.5 %fusion.16 = bf16[384,576]{0,1:T(8,128)(2,1)S(1)} fusion(bf16[1536,192]{0,1:T(8,128)(2,1)S(1)} %copy-done.3, bf16[1536,192]{0,1:T(8,128)(2,1)S(1)} %copy-done.4, bf16[1536,192]{0,1:T(8,128)(2,1)S(1)} %copy-done.5, bf16[384,1536]{1,0:T(8,128)(2,1)} %all-gather.3.cloned.1.call-done, f32[384]{0:T(512)S(1)} %add_rsqrt_fusion, f32[384]{0:T(512)S(1)} %broadcast_multiply_fusion), kind=kOutput, calls=%fused_computation.21 | convolution fusion | flops 687366144 | bytes 3394560 | tf_op jit(solution)/shard_map/dot_general | solution.py:98
  92.7 0.7 slice.23
  93.4 0.0 all-gather.5.cloned.1.call-update
  93.4 0.2 reduce-scatter.2.cloned.1.call-start
  93.7 0.0 copy-done.6
  93.7 0.2 reduce-window.4
  93.9 0.1 convert_reduce_fusion.2
  94.0 0.1 convert_reduce_fusion.1
  94.1 1.5 broadcast_compare_fusion
  95.6 58.5 %all-gather.5.cloned.1.call-done = bf16[6144,384]{0,1:T(8,128)(2,1)} async-done(((bf16[384,384]{0,1:T(8,128)(2,1)}), bf16[6144,384]{0,1:T(8,128)(2,1)}) %all-gather.5.cloned.1.call-update) | async-done | bytes 4718608 | tf_op jit(solution)/shard_map/all_gather | solution.py:109
  154.1 5.1 %fusion.35 = (bf16[6144,192]{0,1:T(8,128)(2,1)}, bf16[6144,192]{0,1:T(8,128)(2,1)}) fusion(bf16[6144,384]{0,1:T(8,128)(2,1)} %all-gather.5.cloned.1.call-done), kind=kLoop, calls=%fused_computation.40 | loop fusion | bytes 9437184 | tf_op jit(solution)/shard_map/slice | solution.py:114
  159.2 6.1 %fusion = (f32[2,384]{1,0:T(2,128)S(1)}, f32[2,384,6144]{2,1,0:T(8,128)S(1)}) fusion(pred[384,6144]{1,0:T(8,128)(4,1)S(1)} %broadcast_compare_fusion, bf16[384,2,96]{0,2,1:T(8,128)(2,1)S(1)} %bitcast.23, bf16[6144,2,96]{0,2,1:T(8,128)(2,1)} %bitcast.22), kind=kOutput, calls=%fused_computation.2 | convolution fusion | flops 920124672 | bytes 23743488 | tf_op jit(solution)/shard_map/qhd,khd->hqk/dot_general | solution.py:116
  165.3 0.0 copy-start.1
  165.3 6.5 %fusion.1 = f32[2,384]{1,0:T(2,128)S(1)} fusion(f32[2,384,6144]{2,1,0:T(8,128)S(1)} %get-tuple-element.8, f32[2,384]{1,0:T(2,128)S(1)} %broadcast_maximum_fusion, pred[384,6144]{1,0:T(8,128)(4,1)S(1)} %broadcast_compare_fusion), kind=kLoop, calls=%fused_computation.3 | loop fusion | flops 23592192 | bytes 21239808 | tf_op jit(solution)/shard_map/reduce_sum | solution.py:120
  171.8 0.0 copy-done.1
  171.8 0.0 copy-start.2
  171.8 10.1 %fusion.28 = bf16[384,2,96]{0,2,1:T(8,128)(2,1)S(1)} fusion(bf16[6144,2,96]{0,2,1:T(8,128)(2,1)} %bitcast.21, f32[2,384,6144]{2,1,0:T(8,128)} %copy-done.1, f32[2,384]{1,0:T(2,128)S(1)} %broadcast_maximum_fusion, pred[384,6144]{1,0:T(8,128)(4,1)S(1)} %broadcast_compare_fusion, f32[384,2]{0,1:T(2,128)S(1)} %bitcast.25), kind=kOutput, calls=%fused_computation.26 | convolution fusion | flops 929710080 | bytes 23746560 | tf_op jit(solution)/shard_map/hqk,khd->hqd/dot_general | solution.py:121
  181.9 0.0 copy-done
  181.9 1.5 convolution_convert_fusion
  183.4 0.0 reduce-scatter.2.cloned.1.call-update
  183.4 38.5 %reduce-scatter.2.cloned.1.call-done = bf16[48,1536]{1,0:T(8,128)(2,1)} async-done(((bf16[384,1536]{1,0:T(8,128)(2,1)}), bf16[48,1536]{1,0:T(8,128)(2,1)}) %reduce-scatter.2.cloned.1.call-update) | async-done | bytes 147472 | tf_op jit(solution)/shard_map/reduce_scatter | solution.py:130
  221.9 0.0 copy-done.2
  221.9 1.6 add_convert_fusion
  (6 shorter events, 0.0 us)
Async XLA Ops:
  6.5 175.4 %copy-start = (bf16[192,1536]{1,0:T(8,128)(2,1)S(1)}, bf16[192,1536]{1,0:T(8,128)(2,1)}, u32[]{:S(2)}) copy-start(bf16[192,1536]{1,0:T(8,128)(2,1)} %param.18) | copy-start | bytes 1769476
  6.5 80.4 %all-gather.3.cloned.1.call-start = ((), (), s32[]{:S(2)}) async-start(), calls=%async_computation.1 | async-start | bytes 1327104 | tf_op jit(solution)/shard_map/all_gather | solution.py:99
  6.5 83.6 %copy-start.3 = (bf16[1536,192]{0,1:T(8,128)(2,1)S(1)}, bf16[1536,192]{0,1:T(8,128)(2,1)}, u32[]{:S(2)}) copy-start(bf16[1536,192]{0,1:T(8,128)(2,1)} %param.17) | copy-start | bytes 1769476
  6.5 83.6 %copy-start.4 = (bf16[1536,192]{0,1:T(8,128)(2,1)S(1)}, bf16[1536,192]{0,1:T(8,128)(2,1)}, u32[]{:S(2)}) copy-start(bf16[1536,192]{0,1:T(8,128)(2,1)} %param.16) | copy-start | bytes 1769476
  6.5 83.6 %copy-start.5 = (bf16[1536,192]{0,1:T(8,128)(2,1)S(1)}, bf16[1536,192]{0,1:T(8,128)(2,1)}, u32[]{:S(2)}) copy-start(bf16[1536,192]{0,1:T(8,128)(2,1)} %param.15) | copy-start | bytes 1769476
  45.2 108.9 %all-gather.5.cloned.1.call-start = ((), (), s32[]{:S(2)}) async-start(), calls=%async_computation.2 | async-start | bytes 5013504 | tf_op jit(solution)/shard_map/all_gather | solution.py:109
  90.2 3.5 %copy-start.6 = (s32[4]{0:T(128)S(1)}, s32[4]{0:T(128)}, u32[]{:S(2)}) copy-start(s32[4]{0:T(128)} %param.19) | copy-start | bytes 52
  93.4 128.5 %reduce-scatter.2.cloned.1.call-start = ((), (), s32[]{:S(2)}) async-start(), calls=%async_computation.3 | async-start | bytes 1327104 | tf_op jit(solution)/shard_map/reduce_scatter | solution.py:130
  165.3 6.5 %copy-start.1 = (f32[2,384,6144]{2,1,0:T(8,128)}, f32[2,384,6144]{2,1,0:T(8,128)S(1)}, u32[]{:S(2)}) copy-start(f32[2,384,6144]{2,1,0:T(8,128)S(1)} %get-tuple-element.8) | copy-start | bytes 56623108
  171.8 50.1 %copy-start.2 = (bf16[48,1536]{1,0:T(8,128)(2,1)S(1)}, bf16[48,1536]{1,0:T(8,128)(2,1)}, u32[]{:S(2)}) copy-start(bf16[48,1536]{1,0:T(8,128)(2,1)} %encode.1) | copy-start | bytes 442372
Sparse Core Ops, SparseCore 0:
  45.3 41.5 all-gather.2
  93.6 60.4 all-gather.4
  183.6 38.3 reduce-scatter.1

commit v2 on v1

--- a/solution.py
+++ b/solution.py
@@ -76,6 +76,16 @@
     )(tiles, w_reduce, w_spatial.reshape(3, 3 * MID, MID), w_expand, w_embed)
 
 
+E = 1536
+HEADS = 16
+TILE_DEV = 8
+BLK_DEV = 16
+PER_DEV = 48
+BLK_ROWS = PER_DEV * TILE_DEV
+NEG = -1e30
+MESH = pl.DeviceIdType.MESH
+
+
 def normalize(rows):
     values = rows.astype(jnp.float32)
     center = jnp.mean(values, axis=1, keepdims=True)
@@ -83,57 +93,169 @@
     return ((values - center) * lax.rsqrt(spread + 1e-05)).astype(jnp.bfloat16)
 
 
-def slide_of(positions, slide_tiles):
-    ends = jnp.cumsum(slide_tiles)[:-1]
-    return jnp.sum((positions[:, None] >= ends[None, :]).astype(jnp.int32), axis=1)
+def nt(a, b):
+    return lax.dot_general(a, b, (((1,), (1,)), ((), ())), preferred_element_type=jnp.float32)
+
+
+def post_body(
+    slides, emb_ref, wq_ref, wk_ref, wv_ref, wo_hbm, o_ref,
+    wo_ref, emb_all, q_st, kv_st, q_all, kv_all, top, total, acc, att_st, att_in,
+    local_sem, emb_send, emb_recv, kv_send, kv_recv, q_send, q_recv, att_send, att_recv,
+):
+    t = lax.axis_index("tile")
+    b = lax.axis_index("blk")
+    half = (b // 2) % 2
+    partner = b + 2 - 4 * half
+
+    def remote(src, dst, send, recv, tile, blk):
+        return pltpu.make_async_remote_copy(
+            src_ref=src, dst_ref=dst, send_sem=send, recv_sem=recv,
+            device_id={"tile": tile, "blk": blk}, device_id_type=MESH,
+        )
+
+    load_out = pltpu.make_async_copy(wo_hbm, wo_ref, local_sem)
+    load_out.start()
+    barrier = pltpu.get_barrier_semaphore()
+    for d in range(1, TILE_DEV):
+        pl.semaphore_signal(barrier, inc=1, device_id={"tile": (t + d) % TILE_DEV, "blk": b}, device_id_type=MESH)
+        pl.semaphore_signal(barrier, inc=1, device_id={"tile": (t + d) % TILE_DEV, "blk": partner}, device_id_type=MESH)
+    for d in range(1, BLK_DEV):
+        pl.semaphore_signal(barrier, inc=1, device_id={"tile": t, "blk": (b + d) % BLK_DEV}, device_id_type=MESH)
+    pl.semaphore_wait(barrier, 2 * (TILE_DEV - 1) + BLK_DEV - 1)
+
+    sends = [
+        remote(emb_ref, emb_all.at[t], emb_send.at[d], emb_recv.at[t], (t + d) % TILE_DEV, b)
+        for d in range(1, TILE_DEV)
+    ]
+    for copy in sends:
+        copy.start()
+    emb_all[t] = emb_ref[...]
+    for d in range(1, TILE_DEV):
+        src = (t + d) % TILE_DEV
+        remote(emb_ref, emb_all.at[src], emb_send.at[d], emb_recv.at[src], src, b).wait_recv()
+    normed = normalize(emb_all[...].reshape(BLK_ROWS, E))
+    keys = nt(wk_ref[...], normed).astype(jnp.bfloat16)
+    values = nt(wv_ref[...], normed).astype(jnp.bfloat16)
+    for h in range(2):
+        kv_st[h, 0:HD] = keys[h * HD : (h + 1) * HD]
+        kv_st[h, HD : 2 * HD] = values[h * HD : (h + 1) * HD]
+    for d in range(1, BLK_DEV):
+        to = (b + d) % BLK_DEV
+        copy = remote(kv_st.at[(to // 2) % 2], kv_all.at[b], kv_send.at[d], kv_recv.at[b], t, to)
+        copy.start()
+        sends.append(copy)
+    queries = nt(wq_ref[...], normed).astype(jnp.bfloat16)
+    for h in range(2):
+        q_st[h] = queries[h * HD : (h + 1) * HD]
+    q_copy = remote(q_st.at[1 - half], q_all, q_send, q_recv, t, partner)
+    q_copy.start()
+    sends.append(q_copy)
+    kv_all[b] = kv_st[half]
+
+    at = lax.broadcasted_iota(jnp.int32, (1, 2 * BLK_ROWS), 1)
+    at = jnp.where(at < BLK_ROWS, b * BLK_ROWS + at, partner * BLK_ROWS + at - BLK_ROWS)
+    low, high, end = jnp.zeros_like(at), jnp.zeros_like(at), 0
+    for s in range(4):
+        start, end = end, end + slides[s]
+        inside = at >= start
+        low = jnp.where(inside, start, low)
+        high = jnp.where(inside, end, high)
+    top[...] = jnp.full((1, 2 * BLK_ROWS), NEG, jnp.float32)
+    total[...] = jnp.zeros((1, 2 * BLK_ROWS), jnp.float32)
+    acc[...] = jnp.zeros((HD, 2 * BLK_ROWS), jnp.float32)
+    q_copy.wait_recv()
+    rate = 1.4426950408889634 / math.sqrt(HD)
+
+    def visit(d, carry):
+        src = (b + d) % BLK_DEV
+
+        @pl.when(d > 0)
+        def _():
+            remote(kv_st.at[0], kv_all.at[src], kv_send.at[0], kv_recv.at[src], t, src).wait_recv()
+
+        key = kv_all[src, 0:HD].T
+        both = jnp.concatenate([q_st[half], q_all[...]], axis=1)
+        scores = jnp.dot(key, both, preferred_element_type=jnp.float32) * rate
+        pos = src * BLK_ROWS + lax.broadcasted_iota(jnp.int32, scores.shape, 0)
+        scores = jnp.where((pos >= low) & (pos < high), scores, NEG)
+        old = top[...]
+        new = jnp.maximum(old, jnp.max(scores, axis=0, keepdims=True))
+        weights = jnp.exp2(scores - new)
+        keep = jnp.exp2(old - new)
+        top[...] = new
+        total[...] = total[...] * keep + jnp.sum(weights, axis=0, keepdims=True)
+        acc[...] = acc[...] * keep + jnp.dot(
+            kv_all[src, HD : 2 * HD], weights.astype(jnp.bfloat16), preferred_element_type=jnp.float32
+        )
+        return carry
+
+    lax.fori_loop(0, BLK_DEV, visit, 0)
+
+    att_st[:, HD:128] = jnp.zeros((2 * BLK_ROWS, 128 - HD), jnp.bfloat16)
+    att_st[:, 0:HD] = (acc[...] / total[...]).T.astype(jnp.bfloat16)
+    head = 2 * t + half
+    for d in range(TILE_DEV):
+        to = (t + d) % TILE_DEV
+        for s, blk in enumerate((b, partner)):
+            src = att_st.at[pl.ds(pl.multiple_of(s * BLK_ROWS + to * PER_DEV, PER_DEV), PER_DEV)]
+            if d == 0 and s == 0:
+                att_in[head] = att_st[pl.ds(pl.multiple_of(to * PER_DEV, PER_DEV), PER_DEV), :]
+            else:
+                copy = remote(src, att_in.at[head], att_send.at[2 * d + s], att_recv.at[head], to, blk)
+                copy.start()
+                sends.append(copy)
+    for d in range(TILE_DEV):
+        src = (t + d) % TILE_DEV
+        for s, blk in enumerate((b, partner)):
+            if d + s:
+                from_head = 2 * src + (half if s == 0 else 1 - half)
+                remote(
+                    att_st.at[0:PER_DEV], att_in.at[from_head], att_send.at[0], att_recv.at[from_head], src, blk
+                ).wait_recv()
+    load_out.wait()
+    attended = jnp.concatenate([att_in[h][:, 0:HD] for h in range(HEADS)], axis=1)
+    mixed = jnp.dot(attended, wo_ref[...], preferred_element_type=jnp.float32)
+    o_ref[...] = (emb_ref[...].astype(jnp.float32) + mixed).astype(jnp.bfloat16)
+    for copy in sends:
+        copy.wait_send()
+
+
+def post(slide_tiles, emb, w_query, w_key, w_value, w_out):
+    vmem = pl.BlockSpec(memory_space=pltpu.VMEM)
+    bf = jnp.bfloat16
+    dma = pltpu.SemaphoreType.DMA
+    return pl.pallas_call(
+        post_body,
+        in_specs=[pl.BlockSpec(memory_space=pltpu.SMEM)] + [vmem] * 4 + [pl.BlockSpec(memory_space=pl.ANY)],
+        out_specs=vmem,
+        out_shape=jax.ShapeDtypeStruct((PER_DEV, E), bf),
+        scratch_shapes=[
+            pltpu.VMEM((E, E), bf),
+            pltpu.VMEM((TILE_DEV, PER_DEV, E), bf),
+            pltpu.VMEM((2, HD, BLK_ROWS), bf),
+            pltpu.VMEM((2, 2 * HD, BLK_ROWS), bf),
+            pltpu.VMEM((HD, BLK_ROWS), bf),
+            pltpu.VMEM((BLK_DEV, 2 * HD, BLK_ROWS), bf),
+            pltpu.VMEM((1, 2 * BLK_ROWS), jnp.float32),
+            pltpu.VMEM((1, 2 * BLK_ROWS), jnp.float32),
+            pltpu.VMEM((HD, 2 * BLK_ROWS), jnp.float32),
+            pltpu.VMEM((2 * BLK_ROWS, 128), bf),
+            pltpu.VMEM((HEADS, PER_DEV, 128), bf),
+            dma, dma((8,)), dma((8,)), dma((16,)), dma((16,)), dma, dma, dma((16,)), dma((16,)),
+        ],
+        compiler_params=pltpu.CompilerParams(
+            vmem_limit_bytes=VMEM_LIMIT, collective_id=0, has_side_effects=True
+        ),
+        name="post",
+    )(slide_tiles, emb, w_query.T, w_key.T, w_value.T, w_out)
 
 
 def shards(
     tiles, w_reduce, w_spatial, w_expand, w_embed, w_query, w_key, w_value, w_out, slide_tiles
 ):
+    w_out_all = lax.all_gather(w_out, "tile", axis=0, tiled=True)
     emb = encode(tiles, w_reduce, w_spatial, w_expand, w_embed)
-    width = w_query.shape[1]
-    heads_here = width // HD
-    w_joined = jnp.concatenate([w_query, w_key, w_value], axis=1)
-    joined = jnp.dot(
-        normalize(lax.all_gather(emb, "tile", axis=0, tiled=True)),
-        w_joined,
-        preferred_element_type=jnp.float32,
-    ).astype(jnp.bfloat16)
-    length = joined.shape[0]
-    query = joined[:, :width].reshape(length, heads_here, HD)
-    key_value = joined[:, width:]
-    query_pos = lax.axis_index("blk") * length + jnp.arange(length, dtype=jnp.int32)
-    query_slide = slide_of(query_pos, slide_tiles)
-    scale = 1.0 / math.sqrt(HD)
-    piece = lax.all_gather(key_value, "blk", axis=0, tiled=True)
-    rows = piece.shape[0]
-    key_pos = jnp.arange(rows, dtype=jnp.int32)
-    same = query_slide[:, None] == slide_of(key_pos, slide_tiles)[None, :]
-    top_old = jnp.full((heads_here, length), -1e30, jnp.float32)
-    keys = piece[:, :width].reshape(rows, heads_here, HD)
-    values = piece[:, width:].reshape(rows, heads_here, HD)
-    scores = jnp.einsum("qhd,khd->hqk", query, keys, preferred_element_type=jnp.float32) * scale
-    scores = jnp.where(same[None], scores, -1e30)
-    top_new = jnp.maximum(top_old, jnp.max(scores, axis=2))
-    probs = jnp.where(same[None], jnp.exp(scores - top_new[:, :, None]), 0.0)
-    total_new = jnp.sum(probs, axis=2)
-    accum_new = jnp.einsum(
-        "hqk,khd->hqd", probs.astype(jnp.bfloat16), values, preferred_element_type=jnp.float32
-    )
-    attended = (
-        (accum_new / total_new[:, :, None])
-        .transpose(1, 0, 2)
-        .reshape(length, width)
-        .astype(jnp.bfloat16)
-    )
-    summed = lax.psum_scatter(
-        jnp.dot(attended, w_out, preferred_element_type=jnp.float32).astype(jnp.bfloat16),
-        "tile",
-        scatter_dimension=0,
-        tiled=True,
-    ).astype(jnp.float32)
-    return (emb.astype(jnp.float32) + summed).astype(jnp.bfloat16)
+    return post(slide_tiles, emb, w_query, w_key, w_value, w_out_all)
 
 
 def solution(mesh):

time: 230 us -> 156 us (0.68)
  the two profiles are of different devices: /device:TPU:8 before, /device:TPU:1 now
where the time goes in v2:
time: 156 us
  Pallas kernels  117 us (75%)
  waiting for transfers between devices  24.7 us (16%)
  between operations  13.4 us (9%)
  local copies, waits for them, and re-layouts  1.58 us (1%)
    pallas_call x1, Pallas kernels, post(): pl.pallas_call(post_body, in_specs=[pl.BlockSpec(memory_space=pltpu.SMEM)...  78 us
    pallas_call x1, Pallas kernels, encode(): pl.pallas_call(encode_body, grid=(48 // T,), in_specs=[pl.BlockSpec((T, 8...  38.5 us
    all_gather x1, waiting for transfers between devices, shards(): w_out_all = lax.all_gather(w_out, 'tile', axis=0, tiled=True)  24 us
  transfers between devices with their start and end apart: 1, of which 1 were waited for; matrix products, arithmetic and copies ran while one was open for 0% of the time, Pallas kernels for 25%

profile of v2, /device:TPU:1, one launch (start us, length us, event | category | flops | bytes accessed | tf_op | source)
XLA Modules:
  0.0 156.2 jit_solution(15811366431388448610)
XLA Ops:
  6.5 0.0 all-gather.2.cloned.1.call-start
  6.5 0.7 all-gather.2.cloned.1.call-update
  7.3 38.5 %encode.1.emb_ref = bf16[48,1536]{1,0:T(8,128)(2,1)} custom-call(bf16[48,8,8,2048]{3,2,1,0:T(8,128)(2,1)} %x_ref.1, bf16[2048,512]{1,0:T(8,128)(2,1)} %wr_ref.1, bf16[3,1536,512]{2,1,0:T(8,128)(2,1)} %bitcast.4, bf16[512,2048]{1,0:T(8,128)(2,1)} %wx_ref.1, bf16[2048,1536]{1,0:T(8,128)(2,1)} %we_ref.1), custom_call_target="tpu_custom_call" | custom-call | tf_op jit(solution)/shard_map/encode/pallas_call | solution.py:58
  45.8 24.0 %all-gather.2.cloned.1.call-done.wo_hbm = bf16[1536,1536]{1,0:T(8,128)(2,1)} async-done(((bf16[192,1536]{1,0:T(8,128)(2,1)}), bf16[1536,1536]{1,0:T(8,128)(2,1)}) %all-gather.2.cloned.1.call-update) | async-done | bytes 4718608 | tf_op jit(solution)/shard_map/all_gather | solution.py:256
  69.8 78.0 %post.1 = bf16[48,1536]{1,0:T(8,128)(2,1)} custom-call(s32[4]{0:T(128)} %slides.1, bf16[48,1536]{1,0:T(8,128)(2,1)} %encode.1.emb_ref, bf16[192,1536]{1,0:T(8,128)(2,1)} %bitcast.5, bf16[192,1536]{1,0:T(8,128)(2,1)} %bitcast.6, bf16[192,1536]{1,0:T(8,128)(2,1)} %bitcast.7, bf16[1536,1536]{1,0:T(8,128)(2,1)} %all-gather.2.cloned.1.call-done.wo_hbm), custom_call_target="tpu_custom_call" | custom-call | tf_op jit(solution)/shard_map/post/pallas_call | solution.py:227
  147.8 1.6 %copy.12 = bf16[48,1536]{1,0:T(8,128)(2,1)} copy(bf16[48,1536]{1,0:T(8,128)(2,1)} %post.1) | data formatting | bytes 294912
Async XLA Ops:
  6.5 63.3 %all-gather.2.cloned.1.call-start = ((), (), s32[]{:S(2)}) async-start(), calls=%async_computation | async-start | bytes 5308416 | tf_op jit(solution)/shard_map/all_gather | solution.py:256
Sparse Core Ops, SparseCore 0:
  9.0 60.7 all-gather.1

commit v3 on v0

v3 whole, which is shorter than its diff:
```python
import math

import jax
import jax.numpy as jnp
from jax import lax
from jax.experimental import pallas as pl
from jax.experimental.pallas import tpu as pltpu
from jax.sharding import PartitionSpec as P

C = 2048
MID = 512
HD = 96
E = 1536
HEADS = 16
TILE_DEV = 8
PER_DEV = 48
T = 16
CHUNKS = PER_DEV // T
R = T * 64
LANES = T * TILE_DEV
SHARD = PER_DEV * TILE_DEV
SLOTS = 16
QW = 2 * LANES
NEG = -1e30
RATE = 1.4426950408889634 / math.sqrt(HD)
VMEM_LIMIT = 61 << 20
MESH = pl.DeviceIdType.MESH
BF = jnp.bfloat16
F32 = jnp.float32


def normalize(rows):
    values = rows.astype(F32)
    center = jnp.mean(values, axis=1, keepdims=True)
    spread = jnp.mean((values - center) ** 2, axis=1, keepdims=True)
    return ((values - center) * lax.rsqrt(spread + 1e-05)).astype(BF)


def nt(a, b):
    return lax.dot_general(a, b, (((1,), (1,)), ((), ())), preferred_element_type=F32)


def body(
    slides, tiles, wr_hbm, ws_hbm, wx_hbm, we_hbm, wq_hbm, wk_hbm, wv_hbm, wo_hbm, o_ref,
    x_buf, wr, ws, wx, we, wq, wk, wv, wo, near, pool, emb, emb_all, q_st, kv_st, q_all, kv_all,
    key_slide, top, total, acc, att_st, att_in,
    x_sem, w_sem, own_sem, emb_send, emb_recv, kv_send, kv_recv, q_send, q_recv, att_send, att_recv,
    wo_send, wo_recv,
):
    t = lax.axis_index("tile")
    b = lax.axis_index("blk")
    core = b % 2
    half = (b // 2) % 2
    y = b // 4
    partner = b + 2 - 4 * half
    sibling = b + 1 - 2 * core
    x = t % 4
    z_lo = t // 4
    mine = 2 * y + half

    def remote(src, dst, send, recv, tile, blk):
        return pltpu.make_async_remote_copy(
            src_ref=src, dst_ref=dst, send_sem=send, recv_sem=recv,
            device_id={"tile": tile, "blk": blk}, device_id_type=MESH,
        )

    def load_x(c):
        return pltpu.make_async_copy(tiles.at[pl.ds(c * T, T)], x_buf.at[c % 2], x_sem.at[c % 2])

    weights = [
        pltpu.make_async_copy(a, v, w_sem.at[i])
        for i, (a, v) in enumerate(
            zip((wr_hbm, ws_hbm, wx_hbm, we_hbm, wk_hbm, wv_hbm, wq_hbm), (wr, ws, wx, we, wk, wv, wq))
        )
    ]
    load_x(0).start()
    for copy in weights:
        copy.start()

    def own_rows(p):
        return pltpu.make_async_copy(wo_hbm.at[pl.ds(p * HD, HD)], wo.at[2 * t + p], own_sem.at[p])

    def out_x(d):
        head = 2 * t + core
        rows = wo_hbm.at[pl.ds(core * HD, HD)]
        return remote(rows, wo.at[head], wo_send.at[d], wo_recv.at[head], z_lo * 4 + (x + d) % 4, b)

    def from_x(d):
        src = z_lo * 4 + (x + d) % 4
        head = 2 * src + core
        return remote(wo.at[head], wo.at[head], wo_send.at[0], wo_recv.at[head], src, b)

    z = 2 * half + z_lo

    def out_z(i):
        to = (z + (1 if i < 2 else 3)) % 4
        head = 2 * (z_lo * 4 + i) + core
        return remote(
            wo.at[head], wo.at[head], wo_send.at[4 + i], wo_recv.at[head],
            (to % 2) * 4 + x, y * 4 + (to // 2) * 2 + core,
        )

    def from_z(i):
        src = (z + (3 if i < 2 else 1)) % 4
        head = 2 * ((1 - z_lo) * 4 + i) + core
        return remote(
            wo.at[head], wo.at[head], wo_send.at[0], wo_recv.at[head],
            (src % 2) * 4 + x, y * 4 + (src // 2) * 2 + core,
        )

    def out_core(d):
        head = 2 * ((t + d) % TILE_DEV) + core
        return remote(wo.at[head], wo.at[head], wo_send.at[8 + d], wo_recv.at[head], t, sibling)

    def from_core(d):
        head = 2 * ((t + d) % TILE_DEV) + 1 - core
        return remote(wo.at[head], wo.at[head], wo_send.at[0], wo_recv.at[head], t, sibling)

    def out_emb(c, d):
        return remote(
            emb.at[c], emb_all.at[c, t], emb_send.at[c, d], emb_recv.at[c, t], (t + d) % TILE_DEV, b
        )

    def from_emb(c, d):
        src = (t + d) % TILE_DEV
        return remote(emb.at[c], emb_all.at[c, src], emb_send.at[c, d], emb_recv.at[c, src], src, b)

    def slot_of(c, s):
        return kv_all.at[c, :, pl.ds(pl.multiple_of(s * LANES, LANES), LANES)]

    def out_kv(c, i, same):
        to = ((y + i) % 4) * 4 + core + 2 * (half if same else 1 - half)
        return remote(
            kv_st.at[c, half if same else 1 - half], slot_of(c, mine),
            kv_send.at[c, 2 * i + (0 if same else 1)], kv_recv.at[c, mine], t, to,
        )

    def out_own(c):
        return remote(
            kv_st.at[c, half], slot_of(c, 8 + mine), kv_send.at[c, 0], kv_recv.at[c, 8 + mine], t, sibling
        )

    def from_kv(c, d):
        u = (mine + d) % 8
        return remote(
            kv_st.at[c, 0], slot_of(c, u), kv_send.at[c, 0], kv_recv.at[c, u], t, 2 * u + core
        )

    def pass_on(c, d):
        u = (mine + d) % 8
        return remote(
            slot_of(c, u), slot_of(c, 8 + u), kv_send.at[c, 8 + d], kv_recv.at[c, 8 + u], t, sibling
        )

    def from_sibling(c, u):
        return remote(
            kv_st.at[c, 0], slot_of(c, 8 + u), kv_send.at[c, 0], kv_recv.at[c, 8 + u], t, sibling
        )

    def swap_q(c):
        return remote(
            q_st.at[c], q_all.at[c, :, LANES:QW], q_send.at[c], q_recv.at[c], t, partner
        )

    barrier = pltpu.get_barrier_semaphore()
    for d in range(1, TILE_DEV):
        for blk in (b, partner):
            pl.semaphore_signal(
                barrier, inc=1, device_id={"tile": (t + d) % TILE_DEV, "blk": blk}, device_id_type=MESH
            )
    for d in range(1, 8):
        pl.semaphore_signal(
            barrier, inc=1, device_id={"tile": t, "blk": 2 * ((mine + d) % 8) + core}, device_id_type=MESH
        )
    pl.semaphore_signal(barrier, inc=1, device_id={"tile": t, "blk": sibling}, device_id_type=MESH)

    near[:, 0] = jnp.zeros((T, 8, 3 * MID), BF)
    near[:, 9] = jnp.zeros((T, 8, 3 * MID), BF)
    for h in range(2):
        own_rows(h).start()

    pl.semaphore_wait(barrier, 2 * (TILE_DEV - 1) + 8)
    for d in range(1, 4):
        out_x(d).start()

    ends = [slides[0], slides[0] + slides[1], slides[0] + slides[1] + slides[2]]

    def slide_at(pos):
        return sum((pos >= end).astype(jnp.int32) for end in ends)

    def table(i, carry):
        n = lax.broadcasted_iota(jnp.int32, (512, 128), 0) + 512 * (i % 4)
        slot = n >> 7
        blk = 2 * (slot & 7) + jnp.where(slot < 8, core, 1 - core)
        pos = blk * SHARD + ((n >> 4) & 7) * PER_DEV + (i // 4) * T + (n & 15)
        key_slide[pl.ds(pl.multiple_of(i * 512, 512), 512), :] = slide_at(pos)
        return carry

    n = lax.broadcasted_iota(jnp.int32, (8, CHUNKS * QW), 1)
    query_pos = (
        jnp.where(((n >> 7) & 1) == 0, b, partner) * SHARD + ((n >> 4) & 7) * PER_DEV + (n >> 8) * T + (n & 15)
    )
    query_slide = slide_at(query_pos)[0:1]
    top[...] = jnp.full((1, CHUNKS * QW), NEG, F32)
    total[...] = jnp.zeros((1, CHUNKS * QW), F32)
    acc[...] = jnp.zeros((HD, CHUNKS * QW), F32)

    def project(c):
        for d in range(1, TILE_DEV):
            from_emb(c, d).wait_recv()
        normed = normalize(emb_all[c].reshape(LANES, E))
        keys = nt(wk[...], normed).astype(BF)
        values = nt(wv[...], normed).astype(BF)
        for h in range(2):
            kv_st[c, h, 0:HD] = keys[h * HD : (h + 1) * HD]
            kv_st[c, h, HD : 2 * HD] = values[h * HD : (h + 1) * HD]
        for i in range(4):
            out_kv(c, i, False).start()
            if i:
                out_kv(c, i, True).start()
        out_own(c).start()
        kv_all[c, :, pl.ds(pl.multiple_of(mine * LANES, LANES), LANES)] = kv_st[c, half]
        queries = nt(wq[...], normed).astype(BF)
        first, second = queries[0:HD], queries[HD : 2 * HD]
        q_all[c, :, 0:LANES] = jnp.where(half == 0, first, second)
        q_st[c] = jnp.where(half == 0, second, first)
        swap_q(c).start()

    def relay(c):
        for d in range(1, 8):
            from_kv(c, d).wait_recv()
            pass_on(c, d).start()

    def attend(c, group, first, last):
        lanes = slice(first * QW, last * QW)
        at = pl.ds(pl.multiple_of(group * 512, 512), 512)
        key = kv_all[c, 0:HD, at].T
        query = jnp.concatenate([q_all[i] for i in range(first, last)], axis=1)
        scores = jnp.dot(key, query, preferred_element_type=F32) * RATE
        slide = key_slide[pl.ds(pl.multiple_of(c * 2048 + group * 512, 512), 512), :]
        slide = jnp.concatenate([slide] * ((last - first) * 2), axis=1)
        scores = jnp.where(slide == query_slide[:, lanes], scores, NEG)
        old = top[:, lanes]
        new = jnp.maximum(old, jnp.max(scores, axis=0, keepdims=True))
        weights = jnp.exp2(scores - new)
        keep = jnp.exp2(old - new)
        top[:, lanes] = new
        total[:, lanes] = total[:, lanes] * keep + jnp.sum(weights, axis=0, keepdims=True)
        acc[:, lanes] = acc[:, lanes] * keep + jnp.dot(
            kv_all[c, HD : 2 * HD, at], weights.astype(BF), preferred_element_type=F32
        )

    def encode(c, carry):
        load_x(c).wait()

        @pl.when(c < CHUNKS - 1)
        def _():
            load_x(c + 1).start()

        def first_use(i):
            @pl.when(c == 0)
            def _():
                weights[i].wait()

        first_use(0)
        x_ref = x_buf.at[c % 2]
        r = jnp.maximum(jnp.dot(x_ref[...].reshape(R, C), wr[...], preferred_element_type=F32), 0.0)
        j = lax.broadcasted_iota(jnp.int32, (R, MID), 0) % 8
        left = jnp.where(j == 0, 0.0, pltpu.roll(r, 1, 0))
        right = jnp.where(j == 7, 0.0, pltpu.roll(r, R - 1, 0))
        for at, shifted in enumerate((left, r, right)):
            near[:, 1:9, :, at * MID : (at + 1) * MID] = shifted.astype(BF).reshape(T, 8, 8, MID)
        first_use(1)
        conv = sum(
            jnp.dot(near[:, k : k + 8].reshape(R, 3 * MID), ws[k], preferred_element_type=F32) for k in range(3)
        )
        s = jnp.maximum(conv, 0.0).astype(BF)
        first_use(2)
        for k in range(4):
            cols = slice(k * 512, (k + 1) * 512)
            out = jnp.dot(s, wx[:, cols], preferred_element_type=F32)
            out = jnp.maximum(out + x_ref[:, :, :, cols].reshape(R, 512).astype(F32), 0.0)
            pool[:, cols] = (jnp.sum(jnp.sum(out.reshape(T, 8, 8, 512), axis=1), axis=1) * (1.0 / 64)).astype(BF)
        first_use(3)
        emb[c] = jnp.dot(pool[...], we[...], preferred_element_type=F32).astype(BF)
        for d in range(1, TILE_DEV):
            out_emb(c, d).start()
        emb_all[c, t] = emb[c]

        @pl.when(c == 0)
        def _():
            for i in range(4, 7):
                weights[i].wait()
            for h in range(2):
                own_rows(h).wait()
            for d in range(1, 4):
                from_x(d).wait_recv()
            for i in range(4):
                out_z(i).start()

        @pl.when(c > 0)
        def _():
            project(c - 1)

        @pl.when(c == 1)
        def _():
            for i in range(4):
                from_z(i).wait_recv()
            for d in range(1, TILE_DEV):
                out_core(d).start()

        return carry

    lax.fori_loop(0, CHUNKS, encode, 0)

    lax.fori_loop(0, 12, table, 0)
    relay(0)
    for c in range(2):
        swap_q(c).wait_recv()
    for u in range(8):
        from_sibling(0, u).wait_recv()
    lax.fori_loop(0, 4, lambda g, k: (attend(0, g, 0, 2), k)[1], 0)
    project(2)
    relay(1)
    swap_q(2).wait_recv()
    lax.fori_loop(0, 4, lambda g, k: (attend(0, g, 2, 3), k)[1], 0)
    for u in range(8):
        from_sibling(1, u).wait_recv()
    lax.fori_loop(0, 4, lambda g, k: (attend(1, g, 0, 3), k)[1], 0)
    relay(2)
    lax.fori_loop(0, 2, lambda g, k: (attend(2, g, 0, 3), k)[1], 0)
    for u in range(8):
        from_sibling(2, u).wait_recv()
    lax.fori_loop(2, 4, lambda g, k: (attend(2, g, 0, 3), k)[1], 0)

    result = (acc[...] / total[...]).T.astype(BF)
    att_st[...] = jnp.concatenate(
        [result, jnp.zeros((CHUNKS * QW, 128 - HD), BF)], axis=1
    ).reshape(CHUNKS, 2, TILE_DEV, T, 128)
    head = 2 * t + half

    def out_att(d, s):
        to = (t + d) % TILE_DEV
        return remote(
            att_st.at[:, s, to], att_in.at[head], att_send.at[2 * d + s], att_recv.at[head], to,
            partner if s else b,
        )

    def from_att(d, s):
        src = (t + d) % TILE_DEV
        other = 2 * src + (1 - half if s else half)
        return remote(
            att_st.at[:, s, 0], att_in.at[other], att_send.at[0], att_recv.at[other], src, partner if s else b
        )

    pairs = [(d, s) for d in range(TILE_DEV) for s in range(2) if d + s]
    for d, s in pairs:
        out_att(d, s).start()
    att_in[head] = att_st[:, 0, t]
    for d in range(1, TILE_DEV):
        from_core(d).wait_recv()
    for d, s in pairs:
        from_att(d, s).wait_recv()
    attended = jnp.concatenate([att_in[h].reshape(PER_DEV, 128)[:, 0:HD] for h in range(HEADS)], axis=1)
    mixed = jnp.dot(attended, wo[...].reshape(E, E), preferred_element_type=F32)
    o_ref[...] = (emb[...].reshape(PER_DEV, E).astype(F32) + mixed).astype(BF)

    for d, s in pairs:
        out_att(d, s).wait_send()
    for d in range(1, 4):
        out_x(d).wait_send()
    for i in range(4):
        out_z(i).wait_send()
    for d in range(1, TILE_DEV):
        out_core(d).wait_send()
    for c in range(CHUNKS):
        for d in range(1, TILE_DEV):
            out_emb(c, d).wait_send()
        for i in range(4):
            out_kv(c, i, False).wait_send()
            if i:
                out_kv(c, i, True).wait_send()
        out_own(c).wait_send()
        for d in range(1, 8):
            pass_on(c, d).wait_send()
        swap_q(c).wait_send()


def shards(
    tiles, w_reduce, w_spatial, w_expand, w_embed, w_query, w_key, w_value, w_out, slide_tiles
):
    anywhere = pl.BlockSpec(memory_space=pl.ANY)
    dma = pltpu.SemaphoreType.DMA
    vmem = pltpu.VMEM
    width = 2 * HD
    return pl.pallas_call(
        body,
        in_specs=[pl.BlockSpec(memory_space=pltpu.SMEM)] + [anywhere] * 9,
        out_specs=pl.BlockSpec(memory_space=vmem),
        out_shape=jax.ShapeDtypeStruct((PER_DEV, E), BF),
        scratch_shapes=[
            vmem((2, T, 8, 8, C), BF),
            vmem((C, MID), BF),
            vmem((3, 3 * MID, MID), BF),
            vmem((MID, C), BF),
            vmem((C, E), BF),
            vmem((width, E), BF),
            vmem((width, E), BF),
            vmem((width, E), BF),
            vmem((HEADS, HD, E), BF),
            vmem((T, 10, 8, 3 * MID), BF),
            vmem((T, C), BF),
            vmem((CHUNKS, T, E), BF),
            vmem((CHUNKS, TILE_DEV, T, E), BF),
            vmem((CHUNKS, HD, LANES), BF),
            vmem((CHUNKS, 2, width, LANES), BF),
            vmem((CHUNKS, HD, QW), BF),
            vmem((CHUNKS, width, SLOTS * LANES), BF),
            vmem((CHUNKS * SLOTS * LANES, 128), jnp.int32),
            vmem((1, CHUNKS * QW), F32),
            vmem((1, CHUNKS * QW), F32),
            vmem((HD, CHUNKS * QW), F32),
            vmem((CHUNKS, 2, TILE_DEV, T, 128), BF),
            vmem((HEADS, CHUNKS, T, 128), BF),
            dma((2,)), dma((7,)), dma((2,)),
            dma((CHUNKS, 8)), dma((CHUNKS, 8)),
            dma((CHUNKS, 16)), dma((CHUNKS, 16)),
            dma((CHUNKS,)), dma((CHUNKS,)),
            dma((16,)), dma((16,)),
            dma((16,)), dma((16,)),
        ],
        compiler_params=pltpu.CompilerParams(
            vmem_limit_bytes=VMEM_LIMIT, collective_id=0, has_side_effects=True
        ),
        name="slide_step",
    )(
        slide_tiles, tiles, w_reduce, w_spatial.reshape(3, 3 * MID, MID), w_expand, w_embed,
        w_query.T, w_key.T, w_value.T, w_out,
    )


def solution(mesh):
    placed = (
        P(("blk", "tile"), None, None, None),
        P(),
        P(),
        P(),
        P(),
        P(None, "tile"),
        P(None, "tile"),
        P(None, "tile"),
        P("tile", None),
        P(),
    )
    return jax.shard_map(
        shards, mesh=mesh, in_specs=placed, out_specs=P(("blk", "tile"), None), check_vma=False
    )
```

time: 306 us -> 102 us (0.33)
  waiting for transfers between devices: 137 us -> 0 us
  matrix products: 110 us -> 0 us
  Pallas kernels: 0 us -> 100 us
  other arithmetic: 25.6 us -> 0 us
  local copies, waits for them, and re-layouts: 19.4 us -> 1.58 us
  between operations: 13.3 us -> 0.01 us
    dot_general x15 -> x0, matrix products: 110 us -> none  [the longest x8 37.9 us: encode(): jnp.dot(window, w_spatial[tap], preferred_element_type=jnp.float32)]
    pallas_call x0 -> x1, Pallas kernels: none -> 100 us  [shards(): pl.pallas_call(body, in_specs=[pl.BlockSpec(memory_space=pltpu.SMEM)] + [...]
    all_gather x2 -> x0, waiting for transfers between devices: 98.9 us -> none  [the longest x1 57.3 us: shards(): piece = lax.all_gather(key_value, 'blk', axis=0, tiled=True)]
    reduce_scatter x1 -> x0, waiting for transfers between devices: 38.4 us -> none  [shards(): lax.psum_scatter(jnp.dot(attended, w_out, preferred_element_type=jnp.floa...]
    reduce_sum x6 -> x0, other arithmetic: 21 us -> none  [the longest x1 9.51 us: encode(): jnp.sum(output.reshape(count, SIDE * SIDE, C), axis=1) / (SIDE * SIDE)]
    slice x4 -> x0, local copies, waits for them, and re-layouts: 19.4 us -> none  [the longest x1 13.5 us: encode(): padded[:, row_off:row_off + SIDE, col_off:col_off + SIDE, :]]
  transfers between devices with their start and end apart: 3 -> 0, of which waited for: 3 -> 0; matrix products, arithmetic and copies ran while one was open for 1% -> 0% of each run, Pallas kernels for 0% -> 0%
where the time goes in v3:
time: 102 us
  Pallas kernels  100 us (98%)
  local copies, waits for them, and re-layouts  1.58 us (2%)
    pallas_call x1, Pallas kernels, shards(): pl.pallas_call(body, in_specs=[pl.BlockSpec(memory_space=pltpu.SMEM)] + [...  100 us

profile of v3, /device:TPU:8, one launch (start us, length us, event | category | flops | bytes accessed | tf_op | source)
XLA Modules:
  0.0 101.6 jit_solution(11173705715869394269)
XLA Ops:
  0.0 100.0 %slide_step.1 = bf16[48,1536]{1,0:T(8,128)(2,1)} custom-call(s32[4]{0:T(128)} %slides.1, bf16[48,8,8,2048]{3,2,1,0:T(8,128)(2,1)} %tiles.1, bf16[2048,512]{1,0:T(8,128)(2,1)} %wr_hbm.1, bf16[3,1536,512]{2,1,0:T(8,128)(2,1)} %bitcast.4, bf16[512,2048]{1,0:T(8,128)(2,1)} %wx_hbm.1, bf16[2048,1536]{1,0:T(8,128)(2,1)} %we_hbm.1, bf16[192,1536]{1,0:T(8,128)(2,1)} %bitcast.5, ...), custom_call_target="tpu_custom_call" | custom-call | tf_op jit(solution)/shard_map/slide_step/pallas_call | solution.py:396
  100.0 1.6 %copy.12 = bf16[48,1536]{1,0:T(8,128)(2,1)} copy(bf16[48,1536]{1,0:T(8,128)(2,1)} %slide_step.1) | data formatting | bytes 294912

commit v4 on v3

--- a/solution.py
+++ b/solution.py
@@ -42,7 +42,7 @@
 
 def body(
     slides, tiles, wr_hbm, ws_hbm, wx_hbm, we_hbm, wq_hbm, wk_hbm, wv_hbm, wo_hbm, o_ref,
-    x_buf, wr, ws, wx, we, wq, wk, wv, wo, near, pool, emb, emb_all, q_st, kv_st, q_all, kv_all,
+    x_buf, wr, ws, wx, we, wqkv, wo, near, pool, emb, emb_all, q_st, kv_st, q_all, kv_all,
     key_slide, top, total, acc, att_st, att_in,
     x_sem, w_sem, own_sem, emb_send, emb_recv, kv_send, kv_recv, q_send, q_recv, att_send, att_recv,
     wo_send, wo_recv,
@@ -70,7 +70,7 @@
     weights = [
         pltpu.make_async_copy(a, v, w_sem.at[i])
         for i, (a, v) in enumerate(
-            zip((wr_hbm, ws_hbm, wx_hbm, we_hbm, wk_hbm, wv_hbm, wq_hbm), (wr, ws, wx, we, wk, wv, wq))
+            zip((wr_hbm, ws_hbm, wx_hbm, we_hbm, wk_hbm, wv_hbm, wq_hbm), (wr, ws, wx, we, wqkv.at[0], wqkv.at[1], wqkv.at[2]))
         )
     ]
     load_x(0).start()
@@ -209,19 +209,17 @@
         for d in range(1, TILE_DEV):
             from_emb(c, d).wait_recv()
         normed = normalize(emb_all[c].reshape(LANES, E))
-        keys = nt(wk[...], normed).astype(BF)
-        values = nt(wv[...], normed).astype(BF)
+        joined = nt(wqkv[...].reshape(6 * HD, E), normed).astype(BF)
         for h in range(2):
-            kv_st[c, h, 0:HD] = keys[h * HD : (h + 1) * HD]
-            kv_st[c, h, HD : 2 * HD] = values[h * HD : (h + 1) * HD]
+            kv_st[c, h, 0:HD] = joined[h * HD : (h + 1) * HD]
+            kv_st[c, h, HD : 2 * HD] = joined[(2 + h) * HD : (3 + h) * HD]
         for i in range(4):
             out_kv(c, i, False).start()
             if i:
                 out_kv(c, i, True).start()
         out_own(c).start()
         kv_all[c, :, pl.ds(pl.multiple_of(mine * LANES, LANES), LANES)] = kv_st[c, half]
-        queries = nt(wq[...], normed).astype(BF)
-        first, second = queries[0:HD], queries[HD : 2 * HD]
+        first, second = joined[4 * HD : 5 * HD], joined[5 * HD : 6 * HD]
         q_all[c, :, 0:LANES] = jnp.where(half == 0, first, second)
         q_st[c] = jnp.where(half == 0, second, first)
         swap_q(c).start()
@@ -276,6 +274,14 @@
         )
         s = jnp.maximum(conv, 0.0).astype(BF)
         first_use(2)
+
+        @pl.when(c == 1)
+        def _():
+            for d in range(1, 4):
+                from_x(d).wait_recv()
+            for i in range(4):
+                out_z(i).start()
+
         for k in range(4):
             cols = slice(k * 512, (k + 1) * 512)
             out = jnp.dot(s, wx[:, cols], preferred_element_type=F32)
@@ -293,28 +299,24 @@
                 weights[i].wait()
             for h in range(2):
                 own_rows(h).wait()
-            for d in range(1, 4):
-                from_x(d).wait_recv()
-            for i in range(4):
-                out_z(i).start()
+
+        @pl.when(c == CHUNKS - 1)
+        def _():
+            relay(0)
 
         @pl.when(c > 0)
         def _():
             project(c - 1)
 
-        @pl.when(c == 1)
-        def _():
-            for i in range(4):
-                from_z(i).wait_recv()
-            for d in range(1, TILE_DEV):
-                out_core(d).start()
-
         return carry
 
     lax.fori_loop(0, CHUNKS, encode, 0)
 
     lax.fori_loop(0, 12, table, 0)
-    relay(0)
+    for i in range(4):
+        from_z(i).wait_recv()
+    for d in range(1, TILE_DEV):
+        out_core(d).start()
     for c in range(2):
         swap_q(c).wait_recv()
     for u in range(8):
@@ -404,9 +406,7 @@
             vmem((3, 3 * MID, MID), BF),
             vmem((MID, C), BF),
             vmem((C, E), BF),
-            vmem((width, E), BF),
-            vmem((width, E), BF),
-            vmem((width, E), BF),
+            vmem((3, width, E), BF),
             vmem((HEADS, HD, E), BF),
             vmem((T, 10, 8, 3 * MID), BF),
             vmem((T, C), BF),

time: 102 us -> 94.5 us (0.926)
  Pallas kernels: 100 us -> 92.8 us
    pallas_call x1, Pallas kernels: 100 us -> 92.8 us  [shards(): pl.pallas_call(body, in_specs=[pl.BlockSpec(memory_space=pltpu.SMEM)] + [...]
where the time goes in v4:
time: 94.5 us; the launch traced here: 94.3 us
  Pallas kernels  92.8 us (98%)
  local copies, waits for them, and re-layouts  1.58 us (2%)
    pallas_call x1, Pallas kernels, shards(): pl.pallas_call(body, in_specs=[pl.BlockSpec(memory_space=pltpu.SMEM)] + [...  92.8 us

profile of v4, /device:TPU:8, one launch (start us, length us, event | category | flops | bytes accessed | tf_op | source)
XLA Modules:
  0.0 94.3 jit_solution(9923265342944197819)
XLA Ops:
  0.0 92.8 %slide_step.1 = bf16[48,1536]{1,0:T(8,128)(2,1)} custom-call(s32[4]{0:T(128)} %slides.1, bf16[48,8,8,2048]{3,2,1,0:T(8,128)(2,1)} %tiles.1, bf16[2048,512]{1,0:T(8,128)(2,1)} %wr_hbm.1, bf16[3,1536,512]{2,1,0:T(8,128)(2,1)} %bitcast.4, bf16[512,2048]{1,0:T(8,128)(2,1)} %wx_hbm.1, bf16[2048,1536]{1,0:T(8,128)(2,1)} %we_hbm.1, bf16[192,1536]{1,0:T(8,128)(2,1)} %bitcast.5, ...), custom_call_target="tpu_custom_call" | custom-call | tf_op jit(solution)/shard_map/slide_step/pallas_call | solution.py:398
  92.8 1.6 %copy.12 = bf16[48,1536]{1,0:T(8,128)(2,1)} copy(bf16[48,1536]{1,0:T(8,128)(2,1)} %slide_step.1) | data formatting | bytes 294912

commit v5 on v4

--- a/solution.py
+++ b/solution.py
@@ -77,44 +77,40 @@
     for copy in weights:
         copy.start()
 
-    def own_rows(p):
-        return pltpu.make_async_copy(wo_hbm.at[pl.ds(p * HD, HD)], wo.at[2 * t + p], own_sem.at[p])
+    own_rows = pltpu.make_async_copy(wo_hbm.at[pl.ds(core * HD, HD)], wo.at[core, t], own_sem)
 
     def out_x(d):
-        head = 2 * t + core
         rows = wo_hbm.at[pl.ds(core * HD, HD)]
-        return remote(rows, wo.at[head], wo_send.at[d], wo_recv.at[head], z_lo * 4 + (x + d) % 4, b)
+        return remote(rows, wo.at[core, t], wo_send.at[d], wo_recv.at[x], z_lo * 4 + (x + d) % 4, b)
 
     def from_x(d):
-        src = z_lo * 4 + (x + d) % 4
-        head = 2 * src + core
-        return remote(wo.at[head], wo.at[head], wo_send.at[0], wo_recv.at[head], src, b)
+        src = (x + d) % 4
+        there = wo.at[core, z_lo * 4 + src]
+        return remote(there, there, wo_send.at[0], wo_recv.at[src], z_lo * 4 + src, b)
 
     z = 2 * half + z_lo
 
     def out_z(i):
-        to = (z + (1 if i < 2 else 3)) % 4
-        head = 2 * (z_lo * 4 + i) + core
-        return remote(
-            wo.at[head], wo.at[head], wo_send.at[4 + i], wo_recv.at[head],
+        to = (z + (3 if i else 1)) % 4
+        rows = wo.at[core, pl.ds(z_lo * 4 + 2 * i, 2)]
+        return remote(
+            rows, rows, wo_send.at[4 + i], wo_recv.at[4 + i],
             (to % 2) * 4 + x, y * 4 + (to // 2) * 2 + core,
         )
 
     def from_z(i):
-        src = (z + (3 if i < 2 else 1)) % 4
-        head = 2 * ((1 - z_lo) * 4 + i) + core
-        return remote(
-            wo.at[head], wo.at[head], wo_send.at[0], wo_recv.at[head],
+        src = (z + (1 if i else 3)) % 4
+        rows = wo.at[core, pl.ds((1 - z_lo) * 4 + 2 * i, 2)]
+        return remote(
+            rows, rows, wo_send.at[0], wo_recv.at[4 + i],
             (src % 2) * 4 + x, y * 4 + (src // 2) * 2 + core,
         )
 
-    def out_core(d):
-        head = 2 * ((t + d) % TILE_DEV) + core
-        return remote(wo.at[head], wo.at[head], wo_send.at[8 + d], wo_recv.at[head], t, sibling)
-
-    def from_core(d):
-        head = 2 * ((t + d) % TILE_DEV) + 1 - core
-        return remote(wo.at[head], wo.at[head], wo_send.at[0], wo_recv.at[head], t, sibling)
+    def out_core():
+        return remote(wo.at[core], wo.at[core], wo_send.at[6], wo_recv.at[6], t, sibling)
+
+    def from_core():
+        return remote(wo.at[1 - core], wo.at[1 - core], wo_send.at[6], wo_recv.at[6], t, sibling)
 
     def out_emb(c, d):
         return remote(
@@ -135,26 +131,16 @@
             kv_send.at[c, 2 * i + (0 if same else 1)], kv_recv.at[c, mine], t, to,
         )
 
-    def out_own(c):
-        return remote(
-            kv_st.at[c, half], slot_of(c, 8 + mine), kv_send.at[c, 0], kv_recv.at[c, 8 + mine], t, sibling
-        )
-
     def from_kv(c, d):
         u = (mine + d) % 8
         return remote(
             kv_st.at[c, 0], slot_of(c, u), kv_send.at[c, 0], kv_recv.at[c, u], t, 2 * u + core
         )
 
-    def pass_on(c, d):
-        u = (mine + d) % 8
-        return remote(
-            slot_of(c, u), slot_of(c, 8 + u), kv_send.at[c, 8 + d], kv_recv.at[c, 8 + u], t, sibling
-        )
-
-    def from_sibling(c, u):
-        return remote(
-            kv_st.at[c, 0], slot_of(c, 8 + u), kv_send.at[c, 0], kv_recv.at[c, 8 + u], t, sibling
+    def pass_on(c):
+        row = SLOTS // 2 * LANES
+        return remote(
+            kv_all.at[c, :, 0:row], kv_all.at[c, :, row : 2 * row], kv_send.at[c, 8], kv_recv.at[c, 8], t, sibling
         )
 
     def swap_q(c):
@@ -176,8 +162,7 @@
 
     near[:, 0] = jnp.zeros((T, 8, 3 * MID), BF)
     near[:, 9] = jnp.zeros((T, 8, 3 * MID), BF)
-    for h in range(2):
-        own_rows(h).start()
+    own_rows.start()
 
     pl.semaphore_wait(barrier, 2 * (TILE_DEV - 1) + 8)
     for d in range(1, 4):
@@ -217,7 +202,6 @@
             out_kv(c, i, False).start()
             if i:
                 out_kv(c, i, True).start()
-        out_own(c).start()
         kv_all[c, :, pl.ds(pl.multiple_of(mine * LANES, LANES), LANES)] = kv_st[c, half]
         first, second = joined[4 * HD : 5 * HD], joined[5 * HD : 6 * HD]
         q_all[c, :, 0:LANES] = jnp.where(half == 0, first, second)
@@ -227,7 +211,7 @@
     def relay(c):
         for d in range(1, 8):
             from_kv(c, d).wait_recv()
-            pass_on(c, d).start()
+        pass_on(c).start()
 
     def attend(c, group, first, last):
         lanes = slice(first * QW, last * QW)
@@ -279,7 +263,7 @@
         def _():
             for d in range(1, 4):
                 from_x(d).wait_recv()
-            for i in range(4):
+            for i in range(2):
                 out_z(i).start()
 
         for k in range(4):
@@ -297,8 +281,7 @@
         def _():
             for i in range(4, 7):
                 weights[i].wait()
-            for h in range(2):
-                own_rows(h).wait()
+            own_rows.wait()
 
         @pl.when(c == CHUNKS - 1)
         def _():
@@ -313,26 +296,22 @@
     lax.fori_loop(0, CHUNKS, encode, 0)
 
     lax.fori_loop(0, 12, table, 0)
-    for i in range(4):
-        from_z(i).wait_recv()
-    for d in range(1, TILE_DEV):
-        out_core(d).start()
     for c in range(2):
         swap_q(c).wait_recv()
-    for u in range(8):
-        from_sibling(0, u).wait_recv()
+    pass_on(0).wait_recv()
     lax.fori_loop(0, 4, lambda g, k: (attend(0, g, 0, 2), k)[1], 0)
     project(2)
     relay(1)
     swap_q(2).wait_recv()
     lax.fori_loop(0, 4, lambda g, k: (attend(0, g, 2, 3), k)[1], 0)
-    for u in range(8):
-        from_sibling(1, u).wait_recv()
+    pass_on(1).wait_recv()
     lax.fori_loop(0, 4, lambda g, k: (attend(1, g, 0, 3), k)[1], 0)
     relay(2)
+    for i in range(2):
+        from_z(i).wait_recv()
+    out_core().start()
     lax.fori_loop(0, 2, lambda g, k: (attend(2, g, 0, 3), k)[1], 0)
-    for u in range(8):
-        from_sibling(2, u).wait_recv()
+    pass_on(2).wait_recv()
     lax.fori_loop(2, 4, lambda g, k: (attend(2, g, 0, 3), k)[1], 0)
 
     result = (acc[...] / total[...]).T.astype(BF)
@@ -359,22 +338,10 @@
     for d, s in pairs:
         out_att(d, s).start()
     att_in[head] = att_st[:, 0, t]
-    for d in range(1, TILE_DEV):
-        from_core(d).wait_recv()
-    for d, s in pairs:
-        from_att(d, s).wait_recv()
-    attended = jnp.concatenate([att_in[h].reshape(PER_DEV, 128)[:, 0:HD] for h in range(HEADS)], axis=1)
-    mixed = jnp.dot(attended, wo[...].reshape(E, E), preferred_element_type=F32)
-    o_ref[...] = (emb[...].reshape(PER_DEV, E).astype(F32) + mixed).astype(BF)
-
-    for d, s in pairs:
-        out_att(d, s).wait_send()
     for d in range(1, 4):
         out_x(d).wait_send()
-    for i in range(4):
+    for i in range(2):
         out_z(i).wait_send()
-    for d in range(1, TILE_DEV):
-        out_core(d).wait_send()
     for c in range(CHUNKS):
         for d in range(1, TILE_DEV):
             out_emb(c, d).wait_send()
@@ -382,10 +349,18 @@
             out_kv(c, i, False).wait_send()
             if i:
                 out_kv(c, i, True).wait_send()
-        out_own(c).wait_send()
-        for d in range(1, 8):
-            pass_on(c, d).wait_send()
+        pass_on(c).wait_send()
         swap_q(c).wait_send()
+    out_core().wait_send()
+    from_core().wait_recv()
+    for d, s in pairs:
+        from_att(d, s).wait_recv()
+    attended = jnp.concatenate([att_in[2 * k + p].reshape(PER_DEV, 128)[:, 0:HD] for p in range(2) for k in range(TILE_DEV)], axis=1)
+    mixed = jnp.dot(attended, wo[...].reshape(E, E), preferred_element_type=F32)
+    o_ref[...] = (emb[...].reshape(PER_DEV, E).astype(F32) + mixed).astype(BF)
+
+    for d, s in pairs:
+        out_att(d, s).wait_send()
 
 
 def shards(
@@ -407,7 +382,7 @@
             vmem((MID, C), BF),
             vmem((C, E), BF),
             vmem((3, width, E), BF),
-            vmem((HEADS, HD, E), BF),
+            vmem((2, TILE_DEV, HD, E), BF),
             vmem((T, 10, 8, 3 * MID), BF),
             vmem((T, C), BF),
             vmem((CHUNKS, T, E), BF),
@@ -422,7 +397,7 @@
             vmem((HD, CHUNKS * QW), F32),
             vmem((CHUNKS, 2, TILE_DEV, T, 128), BF),
             vmem((HEADS, CHUNKS, T, 128), BF),
-            dma((2,)), dma((7,)), dma((2,)),
+            dma((2,)), dma((7,)), dma,
             dma((CHUNKS, 8)), dma((CHUNKS, 8)),
             dma((CHUNKS, 16)), dma((CHUNKS, 16)),
             dma((CHUNKS,)), dma((CHUNKS,)),

time: 94.5 us -> 94.3 us (level)
  no operation moved by 1% of the time
where the time goes in v5:
time: 94.3 us; the launch traced here: 94.2 us
  Pallas kernels  92.6 us (98%)
  local copies, waits for them, and re-layouts  1.58 us (2%)
    pallas_call x1, Pallas kernels, shards(): pl.pallas_call(body, in_specs=[pl.BlockSpec(memory_space=pltpu.SMEM)] + [...  92.6 us

profile of v5, /device:TPU:8, one launch (start us, length us, event | category | flops | bytes accessed | tf_op | source)
XLA Modules:
  0.0 94.2 jit_solution(8648838049651637072)
XLA Ops:
  0.0 92.6 %slide_step.1 = bf16[48,1536]{1,0:T(8,128)(2,1)} custom-call(s32[4]{0:T(128)} %slides.1, bf16[48,8,8,2048]{3,2,1,0:T(8,128)(2,1)} %tiles.1, bf16[2048,512]{1,0:T(8,128)(2,1)} %wr_hbm.1, bf16[3,1536,512]{2,1,0:T(8,128)(2,1)} %bitcast.4, bf16[512,2048]{1,0:T(8,128)(2,1)} %wx_hbm.1, bf16[2048,1536]{1,0:T(8,128)(2,1)} %we_hbm.1, bf16[192,1536]{1,0:T(8,128)(2,1)} %bitcast.5, ...), custom_call_target="tpu_custom_call" | custom-call | tf_op jit(solution)/shard_map/slide_step/pallas_call | solution.py:373
  92.6 1.6 %copy.12 = bf16[48,1536]{1,0:T(8,128)(2,1)} copy(bf16[48,1536]{1,0:T(8,128)(2,1)} %slide_step.1) | data formatting | bytes 294912

commit v6 on v5

--- a/solution.py
+++ b/solution.py
@@ -190,6 +190,8 @@
     total[...] = jnp.zeros((1, CHUNKS * QW), F32)
     acc[...] = jnp.zeros((HD, CHUNKS * QW), F32)
 
+    lax.fori_loop(0, 12, table, 0)
+
     def project(c):
         for d in range(1, TILE_DEV):
             from_emb(c, d).wait_recv()
@@ -259,6 +261,10 @@
         s = jnp.maximum(conv, 0.0).astype(BF)
         first_use(2)
 
+        @pl.when(c > 0)
+        def _():
+            project(c - 1)
+
         @pl.when(c == 1)
         def _():
             for d in range(1, 4):
@@ -283,36 +289,37 @@
                 weights[i].wait()
             own_rows.wait()
 
-        @pl.when(c == CHUNKS - 1)
-        def _():
-            relay(0)
-
         @pl.when(c > 0)
         def _():
-            project(c - 1)
+            relay(c - 1)
 
         return carry
 
     lax.fori_loop(0, CHUNKS, encode, 0)
 
-    lax.fori_loop(0, 12, table, 0)
+    def sweep(c, first, last, start=0, stop=4):
+        def block(g, carry):
+            attend(c, g, first, last)
+            return carry
+
+        lax.fori_loop(start, stop, block, 0)
+
     for c in range(2):
         swap_q(c).wait_recv()
-    pass_on(0).wait_recv()
-    lax.fori_loop(0, 4, lambda g, k: (attend(0, g, 0, 2), k)[1], 0)
+    for c in range(2):
+        pass_on(c).wait_recv()
+        sweep(c, 0, 2)
     project(2)
-    relay(1)
     swap_q(2).wait_recv()
-    lax.fori_loop(0, 4, lambda g, k: (attend(0, g, 2, 3), k)[1], 0)
-    pass_on(1).wait_recv()
-    lax.fori_loop(0, 4, lambda g, k: (attend(1, g, 0, 3), k)[1], 0)
+    sweep(0, 2, 3)
     relay(2)
+    sweep(1, 2, 3)
     for i in range(2):
         from_z(i).wait_recv()
     out_core().start()
-    lax.fori_loop(0, 2, lambda g, k: (attend(2, g, 0, 3), k)[1], 0)
+    sweep(2, 0, 3, 0, 2)
     pass_on(2).wait_recv()
-    lax.fori_loop(2, 4, lambda g, k: (attend(2, g, 0, 3), k)[1], 0)
+    sweep(2, 0, 3, 2, 4)
 
     result = (acc[...] / total[...]).T.astype(BF)
     att_st[...] = jnp.concatenate(

time: 94.3 us -> 96.8 us (1.027); the launches traced: 94.2 us -> 95.5 us
  Pallas kernels: 92.6 us -> 93.9 us
    pallas_call x1, Pallas kernels: 92.6 us -> 93.9 us  [shards(): pl.pallas_call(body, in_specs=[pl.BlockSpec(memory_space=pltpu.SMEM)] + [...]
where the time goes in v6:
time: 96.8 us; the launch traced here: 95.5 us
  Pallas kernels  93.9 us (97%)
  local copies, waits for them, and re-layouts  1.58 us (2%)
    pallas_call x1, Pallas kernels, shards(): pl.pallas_call(body, in_specs=[pl.BlockSpec(memory_space=pltpu.SMEM)] + [...  93.9 us

profile of v6, /device:TPU:8, one launch (start us, length us, event | category | flops | bytes accessed | tf_op | source)
XLA Modules:
  0.0 95.5 jit_solution(11806849281783626549)
XLA Ops:
  0.0 93.9 %slide_step.1 = bf16[48,1536]{1,0:T(8,128)(2,1)} custom-call(s32[4]{0:T(128)} %slides.1, bf16[48,8,8,2048]{3,2,1,0:T(8,128)(2,1)} %tiles.1, bf16[2048,512]{1,0:T(8,128)(2,1)} %wr_hbm.1, bf16[3,1536,512]{2,1,0:T(8,128)(2,1)} %bitcast.4, bf16[512,2048]{1,0:T(8,128)(2,1)} %wx_hbm.1, bf16[2048,1536]{1,0:T(8,128)(2,1)} %we_hbm.1, bf16[192,1536]{1,0:T(8,128)(2,1)} %bitcast.5, ...), custom_call_target="tpu_custom_call" | custom-call | tf_op jit(solution)/shard_map/slide_step/pallas_call | solution.py:380
  93.9 1.6 %copy.12 = bf16[48,1536]{1,0:T(8,128)(2,1)} copy(bf16[48,1536]{1,0:T(8,128)(2,1)} %slide_step.1) | data formatting | bytes 294912

commit v7 on v6

--- a/solution.py
+++ b/solution.py
@@ -122,7 +122,7 @@
         return remote(emb.at[c], emb_all.at[c, src], emb_send.at[c, d], emb_recv.at[c, src], src, b)
 
     def slot_of(c, s):
-        return kv_all.at[c, :, pl.ds(pl.multiple_of(s * LANES, LANES), LANES)]
+        return kv_all.at[c, s]
 
     def out_kv(c, i, same):
         to = ((y + i) % 4) * 4 + core + 2 * (half if same else 1 - half)
@@ -138,9 +138,8 @@
         )
 
     def pass_on(c):
-        row = SLOTS // 2 * LANES
-        return remote(
-            kv_all.at[c, :, 0:row], kv_all.at[c, :, row : 2 * row], kv_send.at[c, 8], kv_recv.at[c, 8], t, sibling
+        return remote(
+            kv_all.at[c, 0:8], kv_all.at[c, 8:16], kv_send.at[c, 8], kv_recv.at[c, 8], t, sibling
         )
 
     def swap_q(c):
@@ -204,7 +203,7 @@
             out_kv(c, i, False).start()
             if i:
                 out_kv(c, i, True).start()
-        kv_all[c, :, pl.ds(pl.multiple_of(mine * LANES, LANES), LANES)] = kv_st[c, half]
+        kv_all[c, mine] = kv_st[c, half]
         first, second = joined[4 * HD : 5 * HD], joined[5 * HD : 6 * HD]
         q_all[c, :, 0:LANES] = jnp.where(half == 0, first, second)
         q_st[c] = jnp.where(half == 0, second, first)
@@ -217,11 +216,11 @@
 
     def attend(c, group, first, last):
         lanes = slice(first * QW, last * QW)
-        at = pl.ds(pl.multiple_of(group * 512, 512), 512)
-        key = kv_all[c, 0:HD, at].T
+        key = jnp.concatenate([kv_all[c, group * 8 + k, 0:HD] for k in range(8)], axis=1).T
+        value = jnp.concatenate([kv_all[c, group * 8 + k, HD : 2 * HD] for k in range(8)], axis=1)
         query = jnp.concatenate([q_all[i] for i in range(first, last)], axis=1)
         scores = jnp.dot(key, query, preferred_element_type=F32) * RATE
-        slide = key_slide[pl.ds(pl.multiple_of(c * 2048 + group * 512, 512), 512), :]
+        slide = key_slide[pl.ds(pl.multiple_of(c * 2048 + group * 1024, 1024), 1024), :]
         slide = jnp.concatenate([slide] * ((last - first) * 2), axis=1)
         scores = jnp.where(slide == query_slide[:, lanes], scores, NEG)
         old = top[:, lanes]
@@ -231,7 +230,7 @@
         top[:, lanes] = new
         total[:, lanes] = total[:, lanes] * keep + jnp.sum(weights, axis=0, keepdims=True)
         acc[:, lanes] = acc[:, lanes] * keep + jnp.dot(
-            kv_all[c, HD : 2 * HD, at], weights.astype(BF), preferred_element_type=F32
+            value, weights.astype(BF), preferred_element_type=F32
         )
 
     def encode(c, carry):
@@ -297,7 +296,7 @@
 
     lax.fori_loop(0, CHUNKS, encode, 0)
 
-    def sweep(c, first, last, start=0, stop=4):
+    def sweep(c, first, last, start=0, stop=2):
         def block(g, carry):
             attend(c, g, first, last)
             return carry
@@ -317,9 +316,9 @@
     for i in range(2):
         from_z(i).wait_recv()
     out_core().start()
-    sweep(2, 0, 3, 0, 2)
+    attend(2, 0, 0, 3)
     pass_on(2).wait_recv()
-    sweep(2, 0, 3, 2, 4)
+    attend(2, 1, 0, 3)
 
     result = (acc[...] / total[...]).T.astype(BF)
     att_st[...] = jnp.concatenate(
@@ -397,7 +396,7 @@
             vmem((CHUNKS, HD, LANES), BF),
             vmem((CHUNKS, 2, width, LANES), BF),
             vmem((CHUNKS, HD, QW), BF),
-            vmem((CHUNKS, width, SLOTS * LANES), BF),
+            vmem((CHUNKS, SLOTS, width, LANES), BF),
             vmem((CHUNKS * SLOTS * LANES, 128), jnp.int32),
             vmem((1, CHUNKS * QW), F32),
             vmem((1, CHUNKS * QW), F32),

time: 96.8 us -> 94.1 us (0.972)
  Pallas kernels: 93.9 us -> 91.3 us
    pallas_call x1, Pallas kernels: 93.9 us -> 91.3 us  [shards(): pl.pallas_call(body, in_specs=[pl.BlockSpec(memory_space=pltpu.SMEM)] + [...]
where the time goes in v7:
time: 94.1 us; the launch traced here: 92.9 us
  Pallas kernels  91.3 us (97%)
  local copies, waits for them, and re-layouts  1.58 us (2%)
    pallas_call x1, Pallas kernels, shards(): pl.pallas_call(body, in_specs=[pl.BlockSpec(memory_space=pltpu.SMEM)] + [...  91.3 us

profile of v7, /device:TPU:8, one launch (start us, length us, event | category | flops | bytes accessed | tf_op | source)
XLA Modules:
  0.0 92.9 jit_solution(7816467640901147441)
XLA Ops:
  0.0 91.3 %slide_step.1 = bf16[48,1536]{1,0:T(8,128)(2,1)} custom-call(s32[4]{0:T(128)} %slides.1, bf16[48,8,8,2048]{3,2,1,0:T(8,128)(2,1)} %tiles.1, bf16[2048,512]{1,0:T(8,128)(2,1)} %wr_hbm.1, bf16[3,1536,512]{2,1,0:T(8,128)(2,1)} %bitcast.4, bf16[512,2048]{1,0:T(8,128)(2,1)} %wx_hbm.1, bf16[2048,1536]{1,0:T(8,128)(2,1)} %we_hbm.1, bf16[192,1536]{1,0:T(8,128)(2,1)} %bitcast.5, ...), custom_call_target="tpu_custom_call" | custom-call | tf_op jit(solution)/shard_map/slide_step/pallas_call | solution.py:379
  91.3 1.6 %copy.12 = bf16[48,1536]{1,0:T(8,128)(2,1)} copy(bf16[48,1536]{1,0:T(8,128)(2,1)} %slide_step.1) | data formatting | bytes 294912

commit v8 on v7

--- a/solution.py
+++ b/solution.py
@@ -88,6 +88,19 @@
         there = wo.at[core, z_lo * 4 + src]
         return remote(there, there, wo_send.at[0], wo_recv.at[src], z_lo * 4 + src, b)
 
+    def over_x(i):
+        src = z_lo * 4 + (x + (1 if i else 3)) % 4
+        rows = wo.at[core, src, pl.ds(48 * i, 48)]
+        return remote(
+            rows, rows, wo_send.at[7 + i], wo_recv.at[7 + i], z_lo * 4 + (x + (3 if i else 1)) % 4, b
+        )
+
+    def from_over_x(i):
+        rows = wo.at[core, z_lo * 4 + (x + 2) % 4, pl.ds(48 * i, 48)]
+        return remote(
+            rows, rows, wo_send.at[0], wo_recv.at[7 + i], z_lo * 4 + (x + (1 if i else 3)) % 4, b
+        )
+
     z = 2 * half + z_lo
 
     def out_z(i):
@@ -164,7 +177,7 @@
     own_rows.start()
 
     pl.semaphore_wait(barrier, 2 * (TILE_DEV - 1) + 8)
-    for d in range(1, 4):
+    for d in (1, 3):
         out_x(d).start()
 
     ends = [slides[0], slides[0] + slides[1], slides[0] + slides[1] + slides[2]]
@@ -260,14 +273,21 @@
         s = jnp.maximum(conv, 0.0).astype(BF)
         first_use(2)
 
+        @pl.when(c == 0)
+        def _():
+            for d in (1, 3):
+                from_x(d).wait_recv()
+            for i in range(2):
+                over_x(i).start()
+
         @pl.when(c > 0)
         def _():
             project(c - 1)
 
         @pl.when(c == 1)
         def _():
-            for d in range(1, 4):
-                from_x(d).wait_recv()
+            for i in range(2):
+                from_over_x(i).wait_recv()
             for i in range(2):
                 out_z(i).start()
 
@@ -344,9 +364,10 @@
     for d, s in pairs:
         out_att(d, s).start()
     att_in[head] = att_st[:, 0, t]
-    for d in range(1, 4):
+    for d in (1, 3):
         out_x(d).wait_send()
     for i in range(2):
+        over_x(i).wait_send()
         out_z(i).wait_send()
     for c in range(CHUNKS):
         for d in range(1, TILE_DEV):

time: 94.1 us -> 94.7 us (level)
  no operation moved by 1% of the time
where the time goes in v8:
time: 94.7 us; the launch traced here: 92.9 us
  Pallas kernels  91.3 us (96%)
  local copies, waits for them, and re-layouts  1.58 us (2%)
    pallas_call x1, Pallas kernels, shards(): pl.pallas_call(body, in_specs=[pl.BlockSpec(memory_space=pltpu.SMEM)] + [...  91.3 us

profile of v8, /device:TPU:8, one launch (start us, length us, event | category | flops | bytes accessed | tf_op | source)
XLA Modules:
  0.0 92.9 jit_solution(2131218407999305066)
XLA Ops:
  0.0 91.3 %slide_step.1 = bf16[48,1536]{1,0:T(8,128)(2,1)} custom-call(s32[4]{0:T(128)} %slides.1, bf16[48,8,8,2048]{3,2,1,0:T(8,128)(2,1)} %tiles.1, bf16[2048,512]{1,0:T(8,128)(2,1)} %wr_hbm.1, bf16[3,1536,512]{2,1,0:T(8,128)(2,1)} %bitcast.4, bf16[512,2048]{1,0:T(8,128)(2,1)} %wx_hbm.1, bf16[2048,1536]{1,0:T(8,128)(2,1)} %we_hbm.1, bf16[192,1536]{1,0:T(8,128)(2,1)} %bitcast.5, ...), custom_call_target="tpu_custom_call" | custom-call | tf_op jit(solution)/shard_map/slide_step/pallas_call | solution.py:400
  91.3 1.6 %copy.12 = bf16[48,1536]{1,0:T(8,128)(2,1)} copy(bf16[48,1536]{1,0:T(8,128)(2,1)} %slide_step.1) | data formatting | bytes 294912

commit v9 on v8

--- a/solution.py
+++ b/solution.py
@@ -176,9 +176,6 @@
     near[:, 9] = jnp.zeros((T, 8, 3 * MID), BF)
     own_rows.start()
 
-    pl.semaphore_wait(barrier, 2 * (TILE_DEV - 1) + 8)
-    for d in (1, 3):
-        out_x(d).start()
 
     ends = [slides[0], slides[0] + slides[1], slides[0] + slides[1] + slides[2]]
 
@@ -266,19 +263,19 @@
         right = jnp.where(j == 7, 0.0, pltpu.roll(r, R - 1, 0))
         for at, shifted in enumerate((left, r, right)):
             near[:, 1:9, :, at * MID : (at + 1) * MID] = shifted.astype(BF).reshape(T, 8, 8, MID)
+
+        @pl.when(c == 0)
+        def _():
+            pl.semaphore_wait(barrier, 2 * (TILE_DEV - 1) + 8)
+            for d in (1, 3):
+                out_x(d).start()
+
         first_use(1)
         conv = sum(
             jnp.dot(near[:, k : k + 8].reshape(R, 3 * MID), ws[k], preferred_element_type=F32) for k in range(3)
         )
         s = jnp.maximum(conv, 0.0).astype(BF)
         first_use(2)
-
-        @pl.when(c == 0)
-        def _():
-            for d in (1, 3):
-                from_x(d).wait_recv()
-            for i in range(2):
-                over_x(i).start()
 
         @pl.when(c > 0)
         def _():
@@ -307,6 +304,10 @@
             for i in range(4, 7):
                 weights[i].wait()
             own_rows.wait()
+            for d in (1, 3):
+                from_x(d).wait_recv()
+            for i in range(2):
+                over_x(i).start()
 
         @pl.when(c > 0)
         def _():

time: 94.7 us -> 94.5 us (level); the launches traced: 92.9 us -> 93.7 us
  no operation moved by 1% of the time
where the time goes in v9:
time: 94.5 us; the launch traced here: 93.7 us
  Pallas kernels  92.1 us (97%)
  local copies, waits for them, and re-layouts  1.58 us (2%)
    pallas_call x1, Pallas kernels, shards(): pl.pallas_call(body, in_specs=[pl.BlockSpec(memory_space=pltpu.SMEM)] + [...  92.1 us

profile of v9, /device:TPU:8, one launch (start us, length us, event | category | flops | bytes accessed | tf_op | source)
XLA Modules:
  0.0 93.7 jit_solution(5307539661417364640)
XLA Ops:
  0.0 92.1 %slide_step.1 = bf16[48,1536]{1,0:T(8,128)(2,1)} custom-call(s32[4]{0:T(128)} %slides.1, bf16[48,8,8,2048]{3,2,1,0:T(8,128)(2,1)} %tiles.1, bf16[2048,512]{1,0:T(8,128)(2,1)} %wr_hbm.1, bf16[3,1536,512]{2,1,0:T(8,128)(2,1)} %bitcast.4, bf16[512,2048]{1,0:T(8,128)(2,1)} %wx_hbm.1, bf16[2048,1536]{1,0:T(8,128)(2,1)} %we_hbm.1, bf16[192,1536]{1,0:T(8,128)(2,1)} %bitcast.5, ...), custom_call_target="tpu_custom_call" | custom-call | tf_op jit(solution)/shard_map/slide_step/pallas_call | solution.py:401
  92.1 1.6 %copy.12 = bf16[48,1536]{1,0:T(8,128)(2,1)} copy(bf16[48,1536]{1,0:T(8,128)(2,1)} %slide_step.1) | data formatting | bytes 294912
